TPU v7x, 1024 devices: a whole 4x8x16 slice. The times are simulated.
1024 devices in a mesh: expert: 64 (over z, x_hi, core), tensor: 8 (over y), dp: 2 (over x_lo).
Axes of the slice: x: 4 (x_hi: 2, x_lo: 2; x = x_hi * 2 + x_lo), y: 8, z: 16, core: 2. Of those that a mesh axis runs over, the one named last changes fastest.
Arguments:
- attn_out: bfloat16 [8192, 8192], P('expert', ('tensor', 'dp')), may hold values from -6 to 6
- out_weight: bfloat16 [8192, 3584], P(('tensor', 'dp')), may hold values from -0.0625 to 0.0625
- residual: bfloat16 [8192, 3584], P(('expert', 'dp'), 'tensor'), may hold values from -38 to 38
- norm_gain: float32 [3584], replicated, may hold values from 0.25 to 1.75
- gate_weights: bfloat16 [64, 3584, 2048], P('expert', None, 'tensor'), may hold values from -0.09375 to 0.09375
- up_weights: bfloat16 [64, 3584, 2048], P('expert', None, 'tensor'), may hold values from -0.09375 to 0.09375
- down_weights: bfloat16 [64, 2048, 3584], P('expert', 'tensor'), may hold values from -0.125 to 0.125
- routes: int32 [8192, 8], P(('expert', 'dp')), may hold values from 0 to 63, as said below
- gate_values: int32 [8192, 8], P(('expert', 'dp')), may hold values from 1 to 16
Outputs:
- mixed: bfloat16 [8192, 3584], P(('expert', 'dp'), 'tensor')
Inputs may be any that keep to these rules, and one draw needn't show every extreme that they name: `routes`: each row names 8 different experts. In each aligned block of 64 rows (the rows of one device), every expert is named by exactly 8 rows.
All inputs are finite; a program needn't handle non-finite values.
Results may differ from a plain program's by a relative error of at most 0.015.
Values may be sent and summed in bfloat16 or wider, within the bound.
No kernel may reach another device: no remote copies, remote signals or barrier semaphores. Data moves between devices by JAX's collectives and lax.ppermute only.
A program may use at most 64 MiB of HBM per device.

v0:
```python
import jax
import jax.numpy as jnp
from jax import lax
from jax.sharding import PartitionSpec as P

norm_eps = 1e-06
route_scale = 2.5


def body(
    attn_out,
    out_weight,
    residual,
    norm_gain,
    gate_weights,
    up_weights,
    down_weights,
    routes,
    gate_values,
):
    tensor_count = lax.axis_size("tensor")
    dp_count = lax.axis_size("dp")
    expert_count = lax.axis_size("expert")
    group_tokens = attn_out.shape[0]
    model_width = out_weight.shape[1]
    width_part = model_width // tensor_count
    own_tokens = group_tokens // dp_count
    local_experts = gate_weights.shape[0]
    top_count = routes.shape[1]
    expert_total = local_experts * expert_count
    capacity = own_tokens * top_count // expert_total
    slot_total = expert_total * capacity
    local_slots = local_experts * capacity
    partial_value = jnp.dot(attn_out, out_weight, preferred_element_type=jnp.float32)
    arranged = partial_value.reshape(dp_count, own_tokens, tensor_count, width_part).transpose(
        2, 0, 1, 3
    )
    arranged = arranged.reshape(tensor_count * dp_count * own_tokens, width_part)
    attn_part = lax.psum_scatter(
        arranged.astype(jnp.bfloat16), ("tensor", "dp"), scatter_dimension=0, tiled=True
    ).astype(jnp.float32)
    stream = (residual.astype(jnp.float32) + attn_part).astype(jnp.bfloat16)
    flat_expert = routes.reshape(-1)
    onehot = (flat_expert[:, None] == jnp.arange(expert_total, dtype=jnp.int32)[None, :]).astype(
        jnp.int32
    )
    earlier = jnp.cumsum(onehot, axis=0) - onehot
    slot = jnp.sum(onehot * earlier, axis=1)
    target = (flat_expert * capacity + slot).reshape(own_tokens, top_count)
    placed = (target[:, :, None] == jnp.arange(slot_total, dtype=jnp.int32)[None, None, :]).astype(
        jnp.float32
    )
    pick = jnp.sum(placed, axis=1).astype(jnp.bfloat16)
    gate_float = gate_values.astype(jnp.float32)
    mix_weight = (route_scale * gate_float / jnp.sum(gate_float, axis=1, keepdims=True)).astype(
        jnp.bfloat16
    )
    combine = jnp.sum(placed * mix_weight.astype(jnp.float32)[:, :, None], axis=1).astype(
        jnp.bfloat16
    )
    gather_dims = (((0,), (0,)), ((), ()))
    share = local_slots // tensor_count
    tensor_rank = lax.axis_index("tensor")
    full_rows = lax.all_gather(stream, "tensor", axis=1, tiled=True)
    pick_share = lax.dynamic_slice_in_dim(
        pick.reshape(own_tokens, expert_count, local_slots), tensor_rank * share, share, 2
    )
    pick_share = pick_share.reshape(own_tokens, expert_count * share)
    sent = lax.dot_general(
        pick_share, full_rows, gather_dims, preferred_element_type=jnp.float32
    ).astype(jnp.bfloat16)
    sent = sent.reshape(expert_count, share, model_width)
    received = lax.all_to_all(sent, "expert", split_axis=0, concat_axis=0, tiled=True)
    whole = lax.all_gather(received, "tensor", axis=1, tiled=True)
    piece = whole.reshape(expert_count * local_slots, model_width)
    width = piece.shape[1]
    wide = piece.astype(jnp.float32)
    scaled = (
        (wide * norm_gain[None, :])
        .astype(jnp.bfloat16)
        .reshape(expert_count, local_experts, capacity, width)
    )
    gate_acc = jnp.einsum(
        "sjcd,jdf->sjcf", scaled, gate_weights, preferred_element_type=jnp.float32
    )
    up_acc = jnp.einsum("sjcd,jdf->sjcf", scaled, up_weights, preferred_element_type=jnp.float32)
    square_acc = jnp.sum(wide * wide, axis=1).reshape(expert_count, local_experts, capacity)
    gate_acc, up_acc, square_acc = (gate_acc, up_acc, square_acc)
    inverse = lax.rsqrt(square_acc / model_width + norm_eps)[..., None]
    gate = inverse * gate_acc
    up = inverse * up_acc
    hidden = (jax.nn.silu(gate) * up).astype(jnp.bfloat16)
    term = jnp.einsum("jfd,sjcf->dsjc", down_weights, hidden, preferred_element_type=jnp.float32)
    summed = lax.psum_scatter(
        term.reshape(width_part * lax.axis_size("tensor"), slot_total).astype(jnp.bfloat16),
        "tensor",
        scatter_dimension=0,
        tiled=True,
    )
    returned = lax.all_to_all(summed, "expert", split_axis=1, concat_axis=1, tiled=True)
    moe = lax.dot_general(
        returned, combine, (((1,), (1,)), ((), ())), preferred_element_type=jnp.float32
    )
    return (stream.astype(jnp.float32) + moe.T).astype(jnp.bfloat16)


def solution(mesh):
    return jax.shard_map(
        body,
        mesh=mesh,
        in_specs=(
            P("expert", ("tensor", "dp")),
            P(("tensor", "dp"), None),
            P(("expert", "dp"), "tensor"),
            P(),
            P("expert", None, "tensor"),
            P("expert", None, "tensor"),
            P("expert", "tensor", None),
            P(("expert", "dp"), None),
            P(("expert", "dp"), None),
        ),
        out_specs=P(("expert", "dp"), "tensor"),
        check_vma=False,
    )
```

profile of v0, /device:TPU:1, one launch (start us, length us, event | category | flops | bytes accessed | tf_op | source)
XLA Modules:
  0.0 358.3 jit_solution(3116287692328700021)
XLA Ops:
  6.5 3.8 %convolution_convert_fusion.1 = bf16[128,3584]{1,0:T(8,128)(2,1)} fusion(bf16[128,512]{1,0:T(8,128)(2,1)} %param.9, bf16[512,3584]{1,0:T(8,128)(2,1)} %param.10), kind=kOutput, calls=%fused_computation.6 | convolution fusion | flops 470220800 | bytes 4718592 | tf_op jit(solution)/shard_map/dot_general | solution.py:34
  10.4 2.4 convert_element_type.89
  12.7 1.3 copy.51
  14.5 1.2 reduce-window.6
  16.4 0.7 select_reduce_fusion
  17.4 75.1 %reduce-scatter.5.cloned.1.call-done = bf16[64,448]{1,0:T(8,128)(2,1)} async-done(((bf16[1024,448]{1,0:T(8,128)(2,1)}), bf16[64,448]{1,0:T(8,128)(2,1)}) %reduce-scatter.5.cloned.1.call-update) | async-done | bytes 57360 | tf_op jit(solution)/shard_map/reduce_scatter | solution.py:39
  92.4 0.9 fusion.64
  93.3 19.3 %all-gather = bf16[8,448,64]{1,2,0:T(8,128)(2,1)S(1)} all-gather(bf16[1,448,64]{1,2,0:T(8,128)(2,1)S(1)} %fusion.64), channel_id=1, replica_groups=mesh['expert'=64,'tensor'=8,'dp'=2] {'tensor'}, dimensions={0}, use_global_device_ids=true | all-gather | bytes 516096 | tf_op jit(solution)/shard_map/all_gather | solution.py:64
  112.8 0.6 reshape.93
  113.7 0.5 broadcast.56
  114.2 0.9 reduce.3
  115.3 64.5 %all_to_all.17 = bf16[64,2,1792]{2,1,0:T(2,128)(2,1)S(1)} all-to-all(bf16[64,2,1792]{2,1,0:T(2,128)(2,1)S(1)} %reshape.100), channel_id=1, replica_groups=mesh['expert'=64,'tensor'=8,'dp'=2] {'expert'}, dimensions={0} | all-to-all | bytes 917504 | tf_op jit(solution)/shard_map/all_to_all | solution.py:73
  179.7 0.4 reshape.101
  180.1 0.8 copy.62
  181.0 44.8 %all-gather.3.cloned.1.call-done = bf16[64,8,3584]{2,0,1:T(8,128)(2,1)} async-done(((bf16[64,1,3584]{2,0,1:T(8,128)(2,1)}), bf16[64,8,3584]{2,0,1:T(8,128)(2,1)}) %all-gather.3.cloned.1.call-update) | async-done | bytes 3670032 | tf_op jit(solution)/shard_map/all_gather | solution.py:74
  225.8 3.0 fusion
  228.9 2.8 fusion.41
  231.7 1.1 fusion.51
  232.9 3.0 fusion.2
  235.9 5.9 %copy.64 = bf16[3584,512]{1,0:T(8,128)(2,1)} copy(bf16[3584,512]{0,1:T(8,128)(2,1)} %fusion.2) | data formatting | bytes 7340032
  241.8 56.9 %reduce-scatter.7.cloned.1.call-done = bf16[448,512]{1,0:T(8,128)(2,1)} async-done(((bf16[3584,512]{1,0:T(8,128)(2,1)}), bf16[448,512]{1,0:T(8,128)(2,1)}) %reduce-scatter.7.cloned.1.call-update) | async-done | bytes 458768
  298.7 1.2 copy.65
  299.9 51.0 %all_to_all.18 = bf16[448,64,8]{0,2,1:T(8,128)(2,1)S(1)} all-to-all(bf16[448,64,8]{0,2,1:T(8,128)(2,1)S(1)} %bitcast.114), channel_id=1, replica_groups=mesh['expert'=64,'tensor'=8,'dp'=2] {'expert'}, dimensions={1} | all-to-all | bytes 917504 | tf_op jit(solution)/shard_map/all_to_all | solution.py:100
  350.9 0.8 fusion.56
  (44 shorter events, 2.3 us)
Async XLA Ops:
  6.5 226.3 %copy-start = (bf16[1,256,3584]{2,1,0:T(8,128)(2,1)S(1)}, bf16[1,256,3584]{2,1,0:T(8,128)(2,1)}, u32[]{:S(2)}) copy-start(bf16[1,256,3584]{2,1,0:T(8,128)(2,1)} %param.15) | copy-start | bytes 5505028
  6.5 85.9 %reduce-scatter.5.cloned.1.call-start = ((), (), s32[]{:S(2)}) async-start(), calls=%async_computation.4 | async-start | bytes 1114112 | tf_op jit(solution)/shard_map/reduce_scatter | solution.py:39
  10.4 3.8 %copy-start.4 = (s32[64,8]{0,1:T(8,128)S(1)}, s32[64,8]{0,1:T(8,128)}, u32[]{:S(2)}) copy-start(s32[64,8]{0,1:T(8,128)} %param.16) | copy-start | bytes 6148
  10.4 4.0 %copy-start.5 = (s32[64,8]{0,1:T(8,128)S(1)}, s32[64,8]{0,1:T(8,128)}, u32[]{:S(2)}) copy-start(s32[64,8]{0,1:T(8,128)} %param.17) | copy-start | bytes 6148
  10.4 82.1 %copy-start.2 = (bf16[64,448]{1,0:T(8,128)(2,1)S(1)}, bf16[64,448]{1,0:T(8,128)(2,1)}, u32[]{:S(2)}) copy-start(bf16[64,448]{1,0:T(8,128)(2,1)} %param.11) | copy-start | bytes 172036
  14.1 211.7 %all-gather.3.cloned.1.call-start = ((), (), s32[]{:S(2)}) async-start(), calls=%async_computation.5 | async-start | bytes 4128768 | tf_op jit(solution)/shard_map/all_gather | solution.py:74
  179.7 49.1 %copy-start.7 = (f32[3584]{0:T(1024)S(1)}, f32[3584]{0:T(1024)}, u32[]{:S(2)}) copy-start(f32[3584]{0:T(1024)} %param.12) | copy-start | bytes 43012
  181.0 117.7 %reduce-scatter.7.cloned.1.call-start = ((), (), s32[]{:S(2)}) async-start(), calls=%async_computation.6 | async-start | bytes 4128768
  225.8 3.1 copy-start.1
  228.9 2.8 copy-start.6
  241.8 109.1 %copy-start.3 = (bf16[64,448]{1,0:T(8,128)(2,1)S(1)}, bf16[64,448]{1,0:T(8,128)(2,1)}, u32[]{:S(2)}) copy-start(bf16[64,448]{1,0:T(8,128)(2,1)} %reduce-scatter.5.cloned.1.call-done) | copy-start | bytes 172036
Sparse Core Ops, SparseCore 0:
  14.2 78.1 reduce-scatter.4
  181.1 44.6 all-gather.2
  241.9 56.7 reduce-scatter.6
where the time goes:
time: 359 us; the launch traced here: 358 us
  waiting for transfers between devices  177 us (49%)
  blocking collectives  135 us (38%)
  local copies, waits for them, and re-layouts  14.7 us (4%)
  between operations  13.3 us (4%)
  matrix products  11.8 us (3%)
  other arithmetic  6.87 us (2%)
    reduce_scatter x1, waiting for transfers between devices, body(): lax.psum_scatter(arranged.astype(jnp.bfloat16), ('tensor', 'dp'), scatter...  75.1 us
    all_to_all x1, blocking collectives, body(): lax.all_to_all(sent, 'expert', split_axis=0, concat_axis=0, tiled=True)  64.5 us
    unnamed x4, waiting for transfers between devices  56.9 us
    all_to_all x1, blocking collectives, body(): lax.all_to_all(summed, 'expert', split_axis=1, concat_axis=1, tiled=True)  51 us
    all_gather x1, waiting for transfers between devices, body(): whole = lax.all_gather(received, 'tensor', axis=1, tiled=True)  44.8 us
    all_gather x1, blocking collectives, body(): full_rows = lax.all_gather(stream, 'tensor', axis=1, tiled=True)  19.3 us
    unnamed x22, local copies, waits for them, and re-layouts  8.43 us
  transfers between devices with their start and end apart: 3, of which 3 were waited for; matrix products, arithmetic and copies ran while one was open for 1% of the time, Pallas kernels for 0%

commit v1 on v0

v1 whole, which is shorter than its diff:
```python
import functools

import jax
import jax.numpy as jnp
from jax import lax
from jax.experimental import pallas as pl
from jax.experimental.pallas import tpu as pltpu
from jax.sharding import PartitionSpec as P

norm_eps = 1e-06
route_scale = 2.5
bf16 = jnp.bfloat16
f32 = jnp.float32


def mm(a, b, contract=(1, 0)):
    return lax.dot_general(
        a, b, (((contract[0],), (contract[1],)), ((), ())), preferred_element_type=f32
    )


def project_kernel(attn_ref, weight_ref, out_ref):
    own_half = out_ref.shape[2]
    part = out_ref.shape[3] // 2
    value = mm(attn_ref[...], weight_ref[...]).astype(bf16)
    for j in range(2):
        for d in range(out_ref.shape[1]):
            for h in range(2):
                row = (d * 2 + h) * own_half
                out_ref[j, d, :, h * part : (h + 1) * part] = value[
                    row : row + own_half, j * part : (j + 1) * part
                ]


def project(attn_out, out_weight, tensor_count, dp_count):
    rows, depth = attn_out.shape
    width = out_weight.shape[1]
    part = width // tensor_count
    own = rows // dp_count
    return pl.pallas_call(
        project_kernel,
        grid=(tensor_count // 2,),
        in_specs=[
            pl.BlockSpec((rows, depth), lambda s: (0, 0)),
            pl.BlockSpec((depth, 2 * part), lambda s: (0, s)),
        ],
        out_specs=pl.BlockSpec((2, dp_count, own // 2, 2 * part), lambda s: (s, 0, 0, 0)),
        out_shape=jax.ShapeDtypeStruct((tensor_count, dp_count, own // 2, 2 * part), bf16),
        name="project",
    )(attn_out, out_weight)


def slots_of(routes, experts, half):
    own = routes.shape[1]
    expert_row = lax.broadcasted_iota(jnp.int32, (experts, own), 0)
    named = jnp.zeros((experts, own), f32)
    for k in range(routes.shape[0]):
        named = named + jnp.where(routes[k : k + 1, :] == expert_row, 1.0, 0.0)
    before = jnp.where(
        lax.broadcasted_iota(jnp.int32, (own, own), 0)
        < lax.broadcasted_iota(jnp.int32, (own, own), 1),
        1.0,
        0.0,
    ).astype(bf16)
    slot = mm(named.astype(bf16), before)
    row = lax.broadcasted_iota(jnp.int32, (experts * half, experts), 0)
    col = lax.broadcasted_iota(jnp.int32, (experts * half, experts), 1)
    repeat = jnp.where(row // half == col, 1.0, 0.0).astype(bf16)
    slot_rows = mm(repeat, slot.astype(bf16))
    place = (lax.broadcasted_iota(jnp.int32, (experts * half, own), 0) % half).astype(f32)
    return named, repeat, slot_rows, place, expert_row


def dispatch_kernel(experts, parts_ref, residual_ref, routes_ref, stream_ref, sent_ref):
    rows, wide = sent_ref.shape
    part = wide // 2
    half = rows // experts
    total = parts_ref[0].astype(f32)
    for i in range(1, parts_ref.shape[0]):
        total = total + parts_ref[i].astype(f32)
    attn = jnp.concatenate([total[:, :part], total[:, part:]], axis=0)
    stream = (residual_ref[...].astype(f32) + attn).astype(bf16)
    stream_ref[...] = stream
    named, repeat, slot_rows, place, _ = slots_of(routes_ref[...], experts, half)
    named_rows = mm(repeat, named.astype(bf16))
    for h in range(2):
        pick = jnp.where(slot_rows == place + h * half, named_rows, 0.0).astype(bf16)
        sent_ref[:, h * part : (h + 1) * part] = mm(pick, stream).astype(bf16)


def expert_kernel(steps, x_ref, gain_ref, gate_ref, up_ref, down_ref, out_ref, gate_acc, up_acc, square_acc, hidden):
    step = pl.program_id(0)
    part = gate_ref.shape[0]
    rows = x_ref.shape[1]
    width = part * steps

    @pl.when(step == 0)
    def _():
        gate_acc[...] = jnp.zeros_like(gate_acc)
        up_acc[...] = jnp.zeros_like(up_acc)
        square_acc[...] = jnp.zeros_like(square_acc)

    @pl.when(step < steps)
    def _():
        for h in range(2):
            wide = x_ref[0, :, h * part : (h + 1) * part].astype(f32)
            scaled = (wide * gain_ref[0]).astype(bf16)
            at = slice(h * rows, (h + 1) * rows)
            gate_acc[at, :] += mm(scaled, gate_ref[...])
            up_acc[at, :] += mm(scaled, up_ref[...])
            square_acc[at, :] += jnp.sum(wide * wide, axis=1, keepdims=True)

    @pl.when(step == steps - 1)
    def _():
        inverse = lax.rsqrt(square_acc[...] / width + norm_eps)
        gate = inverse * gate_acc[...]
        up = inverse * up_acc[...]
        hidden[...] = (jax.nn.silu(gate) * up).astype(bf16)

    @pl.when(step >= steps)
    def _():
        for h in range(2):
            term = mm(hidden[h * rows : (h + 1) * rows, :], down_ref[...]).astype(bf16)
            for j in range(2):
                out_ref[j, :, h * part : (h + 1) * part] = term[:, j * part : (j + 1) * part]


def expert_layer(x, gain, gate_weights, up_weights, down_weights):
    steps, rows, wide = x.shape
    part = wide // 2
    hidden_width = gate_weights.shape[1]
    return pl.pallas_call(
        functools.partial(expert_kernel, steps),
        grid=(steps + steps // 2,),
        in_specs=[
            pl.BlockSpec((1, rows, wide), lambda s: (jnp.minimum(s, steps - 1), 0, 0)),
            pl.BlockSpec((1, 1, part), lambda s: (jnp.minimum(s, steps - 1), 0, 0)),
            pl.BlockSpec((part, hidden_width), lambda s: (jnp.minimum(s, steps - 1), 0)),
            pl.BlockSpec((part, hidden_width), lambda s: (jnp.minimum(s, steps - 1), 0)),
            pl.BlockSpec((hidden_width, wide), lambda s: (0, jnp.maximum(s - steps, 0))),
        ],
        out_specs=pl.BlockSpec((2, rows, wide), lambda s: (jnp.maximum(s - steps, 0), 0, 0)),
        out_shape=jax.ShapeDtypeStruct((steps, rows, wide), bf16),
        scratch_shapes=[
            pltpu.VMEM((2 * rows, hidden_width), f32),
            pltpu.VMEM((2 * rows, hidden_width), f32),
            pltpu.VMEM((2 * rows, 1), f32),
            pltpu.VMEM((2 * rows, hidden_width), bf16),
        ],
        name="expert_layer",
    )(x, gain.reshape(steps, 1, part), gate_weights, up_weights, down_weights)


def combine_kernel(experts, returned_ref, stream_ref, routes_ref, values_ref, out_ref):
    rows, wide = returned_ref.shape
    part = wide // 2
    half = rows // experts
    routes = routes_ref[...]
    values = values_ref[...].astype(f32)
    mix = (route_scale * values / jnp.sum(values, axis=0, keepdims=True)).astype(bf16).astype(f32)
    _, repeat, slot_rows, place, expert_row = slots_of(routes, experts, half)
    weight = jnp.zeros(expert_row.shape, f32)
    for k in range(routes.shape[0]):
        weight = weight + jnp.where(routes[k : k + 1, :] == expert_row, mix[k : k + 1, :], 0.0)
    weight_rows = mm(repeat, weight.astype(bf16))
    moe = stream_ref[...].astype(f32)
    for h in range(2):
        pick = jnp.where(slot_rows == place + h * half, weight_rows, 0.0).astype(bf16)
        moe = moe + mm(pick, returned_ref[:, h * part : (h + 1) * part], (0, 0))
    out_ref[...] = moe.astype(bf16)


def body(
    attn_out,
    out_weight,
    residual,
    norm_gain,
    gate_weights,
    up_weights,
    down_weights,
    routes,
    gate_values,
):
    tensor_count = lax.axis_size("tensor")
    dp_count = lax.axis_size("dp")
    expert_count = lax.axis_size("expert")
    own_tokens = attn_out.shape[0] // dp_count
    part = out_weight.shape[1] // tensor_count
    half = own_tokens * routes.shape[1] // expert_count // 2
    slot_rows = expert_count * half

    parts = project(attn_out, out_weight, tensor_count, dp_count)
    parts = parts.reshape(tensor_count * dp_count, own_tokens // 2, 2 * part)
    parts = lax.all_to_all(parts, ("tensor", "dp"), split_axis=0, concat_axis=0, tiled=True)

    stream, sent = pl.pallas_call(
        functools.partial(dispatch_kernel, expert_count),
        out_shape=(
            jax.ShapeDtypeStruct((own_tokens, part), bf16),
            jax.ShapeDtypeStruct((slot_rows, 2 * part), bf16),
        ),
        name="dispatch",
    )(parts, residual, routes.T)

    sent = sent.reshape(expert_count, half, 2 * part)
    received = lax.all_to_all(sent, "expert", split_axis=0, concat_axis=0, tiled=True)
    whole = lax.all_gather(received.reshape(slot_rows, 2 * part), "tensor", axis=0, tiled=True)

    term = expert_layer(
        whole.reshape(tensor_count, slot_rows, 2 * part),
        norm_gain,
        gate_weights[0],
        up_weights[0],
        down_weights[0],
    )
    summed = lax.psum_scatter(
        term.reshape(tensor_count * slot_rows, 2 * part), "tensor", scatter_dimension=0, tiled=True
    )
    returned = lax.all_to_all(
        summed.reshape(expert_count, half, 2 * part), "expert", split_axis=0, concat_axis=0, tiled=True
    )
    return pl.pallas_call(
        functools.partial(combine_kernel, expert_count),
        out_shape=jax.ShapeDtypeStruct((own_tokens, part), bf16),
        name="combine",
    )(returned.reshape(slot_rows, 2 * part), stream, routes.T, gate_values.T)


def solution(mesh):
    return jax.shard_map(
        body,
        mesh=mesh,
        in_specs=(
            P("expert", ("tensor", "dp")),
            P(("tensor", "dp"), None),
            P(("expert", "dp"), "tensor"),
            P(),
            P("expert", None, "tensor"),
            P("expert", None, "tensor"),
            P("expert", "tensor", None),
            P(("expert", "dp"), None),
            P(("expert", "dp"), None),
        ),
        out_specs=P(("expert", "dp"), "tensor"),
        check_vma=False,
    )
```

time: 359 us -> 277 us (0.77)
  waiting for transfers between devices: 177 us -> 99.2 us
  Pallas kernels: 0 us -> 22 us
  matrix products: 11.8 us -> 0 us
  local copies, waits for them, and re-layouts: 14.7 us -> 4.7 us
  other arithmetic: 6.87 us -> 0 us
    unnamed x4 -> x2, waiting for transfers between devices: 56.9 us -> 0.03 us
    all_to_all x1 -> x2, blocking collectives: 51 us -> 74.2 us  [the longest x1 48.9 us: body(): lax.all_to_all(summed.reshape(expert_count, half, 2 * part), 'expert', sp...]
    pallas_call x0 -> x4, Pallas kernels: none -> 22 us  [the longest x1 12.6 us: expert_layer(): pl.pallas_call(functools.partial(expert_kernel, steps), grid=(steps + ste...]
    all_gather x1 -> x0, blocking collectives: 19.3 us -> none  [body(): full_rows = lax.all_gather(stream, 'tensor', axis=1, tiled=True)]
    reduce_scatter x1, waiting for transfers between devices: 75.1 us -> 56.9 us  [body(): lax.psum_scatter(term.reshape(tensor_count * slot_rows, 2 * part), 'tenso...]
    dot_general x6 -> x0, matrix products: 11.8 us -> none  [the longest x1 3.82 us: body(): jnp.dot(attn_out, out_weight, preferred_element_type=jnp.float32)]
    unnamed x22 -> x2, local copies, waits for them, and re-layouts: 8.43 us -> 0.01 us
    reshape x1 -> x5, local copies, waits for them, and re-layouts: 0.51 us -> 4.69 us  [the longest x1 1.13 us: body(): sent = sent.reshape(expert_count, half, 2 * part)]
  transfers between devices with their start and end apart: 3 -> 2, of which waited for: 3 -> 2; matrix products, arithmetic and copies ran while one was open for 1% -> 0% of each run, Pallas kernels for 0% -> 0%
where the time goes in v1:
time: 277 us
  blocking collectives  137 us (49%)
  waiting for transfers between devices  99.2 us (36%)
  Pallas kernels  22 us (8%)
  between operations  13.4 us (5%)
  local copies, waits for them, and re-layouts  4.7 us (2%)
    all_to_all x1, blocking collectives, body(): lax.all_to_all(sent, 'expert', split_axis=0, concat_axis=0, tiled=True)  63.2 us
    reduce_scatter x1, waiting for transfers between devices, body(): lax.psum_scatter(term.reshape(tensor_count * slot_rows, 2 * part), 'tenso...  56.9 us
    all_to_all x1, blocking collectives, body(): lax.all_to_all(summed.reshape(expert_count, half, 2 * part), 'expert', sp...  48.9 us
    all_gather x1, waiting for transfers between devices, body(): lax.all_gather(received.reshape(slot_rows, 2 * part), 'tensor', axis=0, t...  42.2 us
    all_to_all x1, blocking collectives, body(): lax.all_to_all(parts, ('tensor', 'dp'), split_axis=0, concat_axis=0, tile...  25.4 us
    pallas_call x1, Pallas kernels, expert_layer(): pl.pallas_call(functools.partial(expert_kernel, steps), grid=(steps + ste...  12.6 us
  transfers between devices with their start and end apart: 2, of which 2 were waited for; matrix products, arithmetic and copies ran while one was open for 0% of the time, Pallas kernels for 0%

profile of v1, /device:TPU:1, one launch (start us, length us, event | category | flops | bytes accessed | tf_op | source)
XLA Modules:
  0.0 276.7 jit_solution(14277030341447571714)
XLA Ops:
  6.5 0.0 all-gather.2.cloned.1.call-start
  6.5 4.6 %project.1 = bf16[8,2,32,896]{3,2,1,0:T(8,128)(2,1)} custom-call(bf16[128,512]{1,0:T(8,128)(2,1)} %attn_ref.1, bf16[512,3584]{1,0:T(8,128)(2,1)} %weight_ref.1), custom_call_target="tpu_custom_call" | custom-call | tf_op jit(solution)/shard_map/project/pallas_call | solution.py:40
  11.1 0.0 copy-start
  11.1 25.4 %all_to_all.15.parts_ref = bf16[16,32,896]{2,1,0:T(8,128)(2,1)} all-to-all(bf16[16,32,896]{2,1,0:T(8,128)(2,1)} %bitcast.9), channel_id=1, replica_groups=mesh['expert'=64,'tensor'=8,'dp'=2] {'tensor','dp'}, dimensions={0} | all-to-all | bytes 1835008 | tf_op jit(solution)/shard_map/all_to_all | solution.py:194
  36.5 2.6 dispatch.1
  39.1 1.1 reshape.25
  40.2 63.2 %all_to_all.16 = bf16[64,4,896]{2,1,0:T(4,128)(2,1)S(1)} all-to-all(bf16[64,4,896]{2,1,0:T(4,128)(2,1)S(1)} %reshape.25), channel_id=1, replica_groups=mesh['expert'=64,'tensor'=8,'dp'=2] {'expert'}, dimensions={0} | all-to-all | bytes 917504 | tf_op jit(solution)/shard_map/all_to_all | solution.py:206
  103.4 0.9 reshape.26
  104.3 0.0 all-gather.2.cloned.1.call-update
  104.3 0.0 reduce-scatter.2.cloned.1.call-start
  104.3 0.0 copy-done
  104.4 0.7 reshape.28.gain_ref
  105.0 42.2 %all-gather.2.cloned.1.call-done = bf16[2048,896]{1,0:T(8,128)(2,1)} async-done(((bf16[256,896]{1,0:T(8,128)(2,1)}), bf16[2048,896]{1,0:T(8,128)(2,1)}) %all-gather.2.cloned.1.call-update) | async-done | bytes 3670032 | tf_op jit(solution)/shard_map/all_gather | solution.py:207
  147.3 12.6 %expert_layer.1 = bf16[8,256,896]{2,1,0:T(8,128)(2,1)} custom-call(bf16[8,256,896]{2,1,0:T(8,128)(2,1)} %bitcast.10, f32[8,1,448]{2,1,0:T(1,128)} %reshape.28.gain_ref, bf16[3584,256]{1,0:T(8,128)(2,1)} %bitcast.11, bf16[3584,256]{1,0:T(8,128)(2,1)} %bitcast.12, bf16[256,3584]{1,0:T(8,128)(2,1)} %bitcast.13), custom_call_target="tpu_custom_call" | custom-call | tf_op jit(solution)/shard_map/expert_layer/pallas_call | solution.py:132
  159.8 0.0 reduce-scatter.2.cloned.1.call-update
  159.9 56.9 %reduce-scatter.2.cloned.1.call-done = bf16[256,896]{1,0:T(8,128)(2,1)} async-done(((bf16[2048,896]{1,0:T(8,128)(2,1)}), bf16[256,896]{1,0:T(8,128)(2,1)}) %reduce-scatter.2.cloned.1.call-update) | async-done | bytes 458768 | tf_op jit(solution)/shard_map/reduce_scatter | solution.py:216
  216.8 1.1 reshape.30
  217.9 48.9 %all_to_all.17 = bf16[64,4,896]{2,1,0:T(4,128)(2,1)S(1)} all-to-all(bf16[64,4,896]{2,1,0:T(4,128)(2,1)S(1)} %reshape.30), channel_id=1, replica_groups=mesh['expert'=64,'tensor'=8,'dp'=2] {'expert'}, dimensions={0} | all-to-all | bytes 917504 | tf_op jit(solution)/shard_map/all_to_all | solution.py:219
  266.8 0.9 reshape.31.returned_ref
  267.6 2.2 combine.1
Async XLA Ops:
  6.5 140.7 %all-gather.2.cloned.1.call-start = ((), (), s32[]{:S(2)}) async-start(), calls=%async_computation.4 | async-start | bytes 4128768 | tf_op jit(solution)/shard_map/all_gather | solution.py:207
  11.1 93.2 %copy-start = (f32[3584]{0:T(1024)S(1)}, f32[3584]{0:T(1024)}, u32[]{:S(2)}) copy-start(f32[3584]{0:T(1024)} %param.12) | copy-start | bytes 43012
  104.3 112.5 %reduce-scatter.2.cloned.1.call-start = ((), (), s32[]{:S(2)}) async-start(), calls=%async_computation.5 | async-start | bytes 4128768 | tf_op jit(solution)/shard_map/reduce_scatter | solution.py:216
Sparse Core Ops, SparseCore 0:
  104.4 42.8 all-gather.1
  160.0 56.7 reduce-scatter.1

commit v2 on v1

--- a/solution.py
+++ b/solution.py
@@ -6,6 +6,7 @@
 from jax.experimental import pallas as pl
 from jax.experimental.pallas import tpu as pltpu
 from jax.sharding import PartitionSpec as P
+
 
 norm_eps = 1e-06
 route_scale = 2.5
@@ -88,11 +89,45 @@
         sent_ref[:, h * part : (h + 1) * part] = mm(pick, stream).astype(bf16)
 
 
-def expert_kernel(steps, x_ref, gain_ref, gate_ref, up_ref, down_ref, out_ref, gate_acc, up_acc, square_acc, hidden):
+def pack_kernel(rank_ref, down_ref, *out_refs):
+    count = len(out_refs)
+    rows, wide = out_refs[0].shape
+    part = wide // 2
+    step = pl.program_id(0)
+    for j in range(2):
+        shift = lax.rem(2 * step + j + count - rank_ref[0], count)
+        for s in range(count):
+
+            @pl.when(shift == s)
+            def _():
+                for h in range(2):
+                    out_refs[s][:, h * part : (h + 1) * part] = down_ref[
+                        h * rows : (h + 1) * rows, j * part : (j + 1) * part
+                    ]
+
+
+def pack_down(down_weights, tensor_count):
+    rows, width = down_weights.shape
+    wide = 2 * (width // tensor_count)
+    rank = lax.axis_index("tensor").astype(jnp.int32).reshape(1)
+    whole = pl.BlockSpec((rows // 2, wide), lambda s, rank_ref: (0, 0))
+    return pl.pallas_call(
+        pack_kernel,
+        grid_spec=pltpu.PrefetchScalarGridSpec(
+            num_scalar_prefetch=1,
+            grid=(tensor_count // 2,),
+            in_specs=[pl.BlockSpec((rows, wide), lambda s, rank_ref: (0, s))],
+            out_specs=[whole] * tensor_count,
+        ),
+        out_shape=[jax.ShapeDtypeStruct((rows // 2, wide), bf16)] * tensor_count,
+        name="pack_down",
+    )(rank, down_weights)
+
+
+def hidden_kernel(steps, x_ref, gain_ref, gate_ref, up_ref, out_ref, gate_acc, up_acc, square_acc):
     step = pl.program_id(0)
     part = gate_ref.shape[0]
     rows = x_ref.shape[1]
-    width = part * steps
 
     @pl.when(step == 0)
     def _():
@@ -100,55 +135,76 @@
         up_acc[...] = jnp.zeros_like(up_acc)
         square_acc[...] = jnp.zeros_like(square_acc)
 
-    @pl.when(step < steps)
-    def _():
-        for h in range(2):
-            wide = x_ref[0, :, h * part : (h + 1) * part].astype(f32)
-            scaled = (wide * gain_ref[0]).astype(bf16)
-            at = slice(h * rows, (h + 1) * rows)
-            gate_acc[at, :] += mm(scaled, gate_ref[...])
-            up_acc[at, :] += mm(scaled, up_ref[...])
-            square_acc[at, :] += jnp.sum(wide * wide, axis=1, keepdims=True)
+    for h in range(2):
+        wide = x_ref[0, :, h * part : (h + 1) * part].astype(f32)
+        scaled = (wide * gain_ref[0]).astype(bf16)
+        at = slice(h * rows, (h + 1) * rows)
+        gate_acc[at, :] += mm(scaled, gate_ref[...])
+        up_acc[at, :] += mm(scaled, up_ref[...])
+        square_acc[at, :] += jnp.sum(wide * wide, axis=1, keepdims=True)
 
     @pl.when(step == steps - 1)
     def _():
-        inverse = lax.rsqrt(square_acc[...] / width + norm_eps)
+        inverse = lax.rsqrt(square_acc[...] / (part * steps) + norm_eps)
         gate = inverse * gate_acc[...]
         up = inverse * up_acc[...]
-        hidden[...] = (jax.nn.silu(gate) * up).astype(bf16)
-
-    @pl.when(step >= steps)
-    def _():
-        for h in range(2):
-            term = mm(hidden[h * rows : (h + 1) * rows, :], down_ref[...]).astype(bf16)
-            for j in range(2):
-                out_ref[j, :, h * part : (h + 1) * part] = term[:, j * part : (j + 1) * part]
-
-
-def expert_layer(x, gain, gate_weights, up_weights, down_weights):
+        out_ref[...] = (jax.nn.silu(gate) * up).astype(bf16)
+
+
+def hidden_units(x, gain, gate_weights, up_weights):
     steps, rows, wide = x.shape
     part = wide // 2
     hidden_width = gate_weights.shape[1]
     return pl.pallas_call(
-        functools.partial(expert_kernel, steps),
-        grid=(steps + steps // 2,),
+        functools.partial(hidden_kernel, steps),
+        grid=(steps,),
         in_specs=[
-            pl.BlockSpec((1, rows, wide), lambda s: (jnp.minimum(s, steps - 1), 0, 0)),
-            pl.BlockSpec((1, 1, part), lambda s: (jnp.minimum(s, steps - 1), 0, 0)),
-            pl.BlockSpec((part, hidden_width), lambda s: (jnp.minimum(s, steps - 1), 0)),
-            pl.BlockSpec((part, hidden_width), lambda s: (jnp.minimum(s, steps - 1), 0)),
-            pl.BlockSpec((hidden_width, wide), lambda s: (0, jnp.maximum(s - steps, 0))),
+            pl.BlockSpec((1, rows, wide), lambda s: (s, 0, 0)),
+            pl.BlockSpec((1, 1, part), lambda s: (s, 0, 0)),
+            pl.BlockSpec((part, hidden_width), lambda s: (s, 0)),
+            pl.BlockSpec((part, hidden_width), lambda s: (s, 0)),
         ],
-        out_specs=pl.BlockSpec((2, rows, wide), lambda s: (jnp.maximum(s - steps, 0), 0, 0)),
-        out_shape=jax.ShapeDtypeStruct((steps, rows, wide), bf16),
+        out_specs=pl.BlockSpec((2 * rows, hidden_width), lambda s: (0, 0)),
+        out_shape=jax.ShapeDtypeStruct((2 * rows, hidden_width), bf16),
         scratch_shapes=[
             pltpu.VMEM((2 * rows, hidden_width), f32),
             pltpu.VMEM((2 * rows, hidden_width), f32),
             pltpu.VMEM((2 * rows, 1), f32),
-            pltpu.VMEM((2 * rows, hidden_width), bf16),
         ],
-        name="expert_layer",
-    )(x, gain.reshape(steps, 1, part), gate_weights, up_weights, down_weights)
+        name="hidden_units",
+    )(x, gain.reshape(steps, 1, part), gate_weights, up_weights)
+
+
+def output_kernel(rank_ref, hidden_ref, *refs):
+    down_refs, out_ref = refs[:-1], refs[-1]
+    count = len(down_refs)
+    rows, wide = out_ref.shape
+    part = wide // 2
+    total = None
+    for s, down_ref in enumerate(down_refs):
+        down = jnp.concatenate([down_ref[:, :part], down_ref[:, part:]], axis=0)
+        term = mm(hidden_ref[lax.rem(rank_ref[0] + count - s, count)], down)
+        total = term if total is None else total + term
+    for h in range(2):
+        out_ref[:, h * part : (h + 1) * part] = total[h * rows : (h + 1) * rows, :].astype(bf16)
+
+
+def expert_outputs(hidden, down):
+    _, rows, _ = hidden.shape
+    _, wide = down[0].shape
+    rank = lax.axis_index("tensor").astype(jnp.int32).reshape(1)
+    return pl.pallas_call(
+        output_kernel,
+        grid_spec=pltpu.PrefetchScalarGridSpec(
+            num_scalar_prefetch=1,
+            grid=(1,),
+            in_specs=[pl.BlockSpec(hidden.shape, lambda i, rank_ref: (0, 0, 0))]
+            + [pl.BlockSpec(d.shape, lambda i, rank_ref: (0, 0)) for d in down],
+            out_specs=pl.BlockSpec((rows // 2, wide), lambda i, rank_ref: (0, 0)),
+        ),
+        out_shape=jax.ShapeDtypeStruct((rows // 2, wide), bf16),
+        name="expert_outputs",
+    )(rank, hidden, *down)
 
 
 def combine_kernel(experts, returned_ref, stream_ref, routes_ref, values_ref, out_ref):
@@ -192,7 +248,7 @@
     parts = project(attn_out, out_weight, tensor_count, dp_count)
     parts = parts.reshape(tensor_count * dp_count, own_tokens // 2, 2 * part)
     parts = lax.all_to_all(parts, ("tensor", "dp"), split_axis=0, concat_axis=0, tiled=True)
-
+    packed = pack_down(down_weights[0], tensor_count)
     stream, sent = pl.pallas_call(
         functools.partial(dispatch_kernel, expert_count),
         out_shape=(
@@ -203,19 +259,24 @@
     )(parts, residual, routes.T)
 
     sent = sent.reshape(expert_count, half, 2 * part)
+    sent, *packed = lax.optimization_barrier((sent, *packed))
     received = lax.all_to_all(sent, "expert", split_axis=0, concat_axis=0, tiled=True)
+    rolled = [
+        lax.ppermute(piece, "tensor", [(i, (i + shift) % tensor_count) for i in range(tensor_count)])
+        if shift
+        else piece
+        for shift, piece in enumerate(packed)
+    ]
     whole = lax.all_gather(received.reshape(slot_rows, 2 * part), "tensor", axis=0, tiled=True)
 
-    term = expert_layer(
+    hidden = hidden_units(
         whole.reshape(tensor_count, slot_rows, 2 * part),
         norm_gain,
         gate_weights[0],
         up_weights[0],
-        down_weights[0],
     )
-    summed = lax.psum_scatter(
-        term.reshape(tensor_count * slot_rows, 2 * part), "tensor", scatter_dimension=0, tiled=True
-    )
+    hidden_all = lax.all_gather(hidden, "tensor", axis=0, tiled=False)
+    summed = expert_outputs(hidden_all, rolled)
     returned = lax.all_to_all(
         summed.reshape(expert_count, half, 2 * part), "expert", split_axis=0, concat_axis=0, tiled=True
     )

time: 277 us -> 300 us (1.083)
  starting transfers between devices: 0.04 us -> 34.5 us
  blocking collectives: 137 us -> 112 us
  waiting for transfers between devices: 99.2 us -> 106 us
  Pallas kernels: 22 us -> 26.7 us
    reduce_scatter x1 -> x0, waiting for transfers between devices: 56.9 us -> none  [body(): lax.psum_scatter(term.reshape(tensor_count * slot_rows, 2 * part), 'tenso...]
    ppermute x0 -> x7, waiting for transfers between devices: none -> 44.8 us  [body(): lax.ppermute(piece, 'tensor', [(i, (i + shift) % tensor_count) for i in r...]
    ppermute x0 -> x7, starting transfers between devices: none -> 25.8 us  [body(): lax.ppermute(piece, 'tensor', [(i, (i + shift) % tensor_count) for i in r...]
    all_to_all x1 -> x0, blocking collectives: 25.4 us -> none  [body(): lax.all_to_all(parts, ('tensor', 'dp'), split_axis=0, concat_axis=0, tile...]
    all_to_all x0 -> x1, waiting for transfers between devices: none -> 11.8 us  [body(): lax.all_to_all(parts, ('tensor', 'dp'), split_axis=0, concat_axis=0, tile...]
    all_to_all x0 -> x1, starting transfers between devices: none -> 8.67 us  [body(): lax.all_to_all(parts, ('tensor', 'dp'), split_axis=0, concat_axis=0, tile...]
    all_gather x0 -> x1, waiting for transfers between devices: none -> 7.6 us  [body(): hidden_all = lax.all_gather(hidden, 'tensor', axis=0, tiled=False)]
    pallas_call x1 -> x3, Pallas kernels: 12.6 us -> 17.3 us  [the longest x1 8.77 us: hidden_units(): pl.pallas_call(functools.partial(hidden_kernel, steps), grid=(steps,), in...]
  transfers between devices with their start and end apart: 2 -> 10, of which waited for: 2 -> 7; matrix products, arithmetic and copies ran while one was open for 0% -> 0% of each run, Pallas kernels for 0% -> 1%
where the time goes in v2:
time: 300 us; the launch traced here: 299 us
  blocking collectives  112 us (37%)
  waiting for transfers between devices  106 us (35%)
  starting transfers between devices  34.5 us (12%)
  Pallas kernels  26.7 us (9%)
  between operations  13.6 us (5%)
  local copies, waits for them, and re-layouts  5.69 us (2%)
    all_to_all x1, blocking collectives, body(): lax.all_to_all(sent, 'expert', split_axis=0, concat_axis=0, tiled=True)  63.8 us
    all_to_all x1, blocking collectives, body(): lax.all_to_all(summed.reshape(expert_count, half, 2 * part), 'expert', sp...  48.3 us
    ppermute x7, waiting for transfers between devices, body(): lax.ppermute(piece, 'tensor', [(i, (i + shift) % tensor_count) for i in r...  44.8 us
    all_gather x1, waiting for transfers between devices, body(): lax.all_gather(received.reshape(slot_rows, 2 * part), 'tensor', axis=0, t...  42 us
    ppermute x7, starting transfers between devices, body(): lax.ppermute(piece, 'tensor', [(i, (i + shift) % tensor_count) for i in r...  25.8 us
    all_to_all x1, waiting for transfers between devices, body(): lax.all_to_all(parts, ('tensor', 'dp'), split_axis=0, concat_axis=0, tile...  11.8 us
    pallas_call x1, Pallas kernels, hidden_units(): pl.pallas_call(functools.partial(hidden_kernel, steps), grid=(steps,), in...  8.77 us
    all_to_all x1, starting transfers between devices, body(): lax.all_to_all(parts, ('tensor', 'dp'), split_axis=0, concat_axis=0, tile...  8.67 us
  transfers between devices with their start and end apart: 10, of which 7 were waited for; matrix products, arithmetic and copies ran while one was open for 0% of the time, Pallas kernels for 1%

profile of v2, /device:TPU:1, one launch (start us, length us, event | category | flops | bytes accessed | tf_op | source)
XLA Modules:
  0.0 298.9 jit_solution(8988274888894554285)
XLA Ops:
  6.5 4.6 %project.1 = bf16[8,2,32,896]{3,2,1,0:T(8,128)(2,1)} custom-call(bf16[128,512]{1,0:T(8,128)(2,1)} %attn_ref.1, bf16[512,3584]{1,0:T(8,128)(2,1)} %weight_ref.1), custom_call_target="tpu_custom_call" | custom-call | tf_op jit(solution)/shard_map/project/pallas_call | solution.py:41
  11.1 8.7 %all-to-all-start = ((bf16[16,32,896]{2,1,0:T(8,128)(2,1)}), bf16[16,32,896]{2,1,0:T(8,128)(2,1)S(1)}, u32[]{:S(2)}, u32[]{:S(2)}) async-start(bf16[16,32,896]{2,1,0:T(8,128)(2,1)} %bitcast.9), calls=%async_computation | async-start | bytes 1835008 | tf_op jit(solution)/shard_map/all_to_all | solution.py:250
  19.8 4.2 %pack_down.1 = (bf16[128,896]{1,0:T(8,128)(2,1)}, bf16[128,896]{1,0:T(8,128)(2,1)}, bf16[128,896]{1,0:T(8,128)(2,1)}, bf16[128,896]{1,0:T(8,128)(2,1)}, bf16[128...) custom-call(s32[1]{0:T(128)} %bitcast.rank_ref, ...), custom_call_target="tpu_custom_call" | custom-call | tf_op jit(solution)/shard_map/pack_down/pallas_call | solution.py:114
  24.0 11.8 %all-to-all-done.parts_ref = bf16[16,32,896]{2,1,0:T(8,128)(2,1)S(1)} async-done(((bf16[16,32,896]{2,1,0:T(8,128)(2,1)}), bf16[16,32,896]{2,1,0:T(8,128)(2,1)S(1)}, u32[]{:S(2)}, u32[]{:S(2)}) %all-to-all-start) | async-done | bytes 917536 | tf_op jit(solution)/shard_map/all_to_all | solution.py:250
  36.8 2.6 dispatch.1
  40.5 63.8 %all_to_all.15 = bf16[64,4,896]{2,1,0:T(4,128)(2,1)S(1)} all-to-all(bf16[64,4,896]{2,1,0:T(4,128)(2,1)S(1)} %reshape.27), channel_id=1, replica_groups=mesh['expert'=64,'tensor'=8,'dp'=2] {'expert'}, dimensions={0} | all-to-all | bytes 917504 | tf_op jit(solution)/shard_map/all_to_all | solution.py:263
  106.0 42.0 %all-gather.4.cloned.1.call-done = bf16[2048,896]{1,0:T(8,128)(2,1)} async-done(((bf16[256,896]{1,0:T(8,128)(2,1)}), bf16[2048,896]{1,0:T(8,128)(2,1)}) %all-gather.4.cloned.1.call-update) | async-done | bytes 3670032 | tf_op jit(solution)/shard_map/all_gather | solution.py:270
  148.0 8.8 %hidden_units.1 = bf16[512,256]{1,0:T(8,128)(2,1)} custom-call(bf16[8,256,896]{2,1,0:T(8,128)(2,1)} %bitcast.10, f32[8,1,448]{2,1,0:T(1,128)} %reshape.30.gain_ref, bf16[3584,256]{1,0:T(8,128)(2,1)} %bitcast.13, bf16[3584,256]{1,0:T(8,128)(2,1)} %bitcast.14), custom_call_target="tpu_custom_call" | custom-call | tf_op jit(solution)/shard_map/hidden_units/pallas_call | solution.py:158
  156.8 1.9 collective-permute-start
  158.8 5.1 %collective-permute-start.1 = (bf16[128,896]{1,0:T(8,128)(2,1)S(1)}, bf16[128,896]{1,0:T(8,128)(2,1)S(1)}, u32[]{:S(2)}, u32[]{:S(2)}) collective-permute-start(bf16[128,896]{1,0:T(8,128)(2,1)S(1)} %copy-done.14), channel_id=1, source_target_pairs={{0,4},{2,6},{4,8},{6,10},{8,12},{10,14},{12,0},{14,2},{1,5},{3,7},... | collective-permute-start | bytes 688136 | tf_op jit(solution)/shard_map/ppermute | solution.py:265
  163.8 3.1 %collective-permute-start.2 = (bf16[128,896]{1,0:T(8,128)(2,1)S(1)}, bf16[128,896]{1,0:T(8,128)(2,1)S(1)}, u32[]{:S(2)}, u32[]{:S(2)}) collective-permute-start(bf16[128,896]{1,0:T(8,128)(2,1)S(1)} %copy-done.13), channel_id=1, source_target_pairs={{0,6},{2,8},{4,10},{6,12},{8,14},{10,0},{12,2},{14,4},{1,7},{3,9},... | collective-permute-start | bytes 688136 | tf_op jit(solution)/shard_map/ppermute | solution.py:265
  167.0 4.2 %collective-permute-start.3 = (bf16[128,896]{1,0:T(8,128)(2,1)S(1)}, bf16[128,896]{1,0:T(8,128)(2,1)S(1)}, u32[]{:S(2)}, u32[]{:S(2)}) collective-permute-start(bf16[128,896]{1,0:T(8,128)(2,1)S(1)} %copy-done.12), channel_id=1, source_target_pairs={{0,8},{2,10},{4,12},{6,14},{8,0},{10,2},{12,4},{14,6},{1,9},{3,11}... | collective-permute-start | bytes 688136 | tf_op jit(solution)/shard_map/ppermute | solution.py:265
  171.2 4.1 %collective-permute-start.4 = (bf16[128,896]{1,0:T(8,128)(2,1)S(1)}, bf16[128,896]{1,0:T(8,128)(2,1)S(1)}, u32[]{:S(2)}, u32[]{:S(2)}) collective-permute-start(bf16[128,896]{1,0:T(8,128)(2,1)S(1)} %copy-done.11), channel_id=1, source_target_pairs={{0,10},{2,12},{4,14},{6,0},{8,2},{10,4},{12,6},{14,8},{1,11},{3,13... | collective-permute-start | bytes 688136 | tf_op jit(solution)/shard_map/ppermute | solution.py:265
  175.4 5.2 %collective-permute-start.5 = (bf16[128,896]{1,0:T(8,128)(2,1)S(1)}, bf16[128,896]{1,0:T(8,128)(2,1)S(1)}, u32[]{:S(2)}, u32[]{:S(2)}) collective-permute-start(bf16[128,896]{1,0:T(8,128)(2,1)S(1)} %copy-done.10), channel_id=1, source_target_pairs={{0,12},{2,14},{4,0},{6,2},{8,4},{10,6},{12,8},{14,10},{1,13},{3,15... | collective-permute-start | bytes 688136 | tf_op jit(solution)/shard_map/ppermute | solution.py:265
  180.6 2.2 collective-permute-start.6
  182.8 9.8 %collective-permute-done.2.refs_3_ = bf16[128,896]{1,0:T(8,128)(2,1)S(1)} collective-permute-done((bf16[128,896]{1,0:T(8,128)(2,1)S(1)}, bf16[128,896]{1,0:T(8,128)(2,1)S(1)}, u32[]{:S(2)}, u32[]{:S(2)}) %collective-permute-start.2) | collective-permute-done | bytes 229408 | tf_op jit(solution)/shard_map/ppermute | solution.py:265
  192.5 13.1 %collective-permute-done.3.refs_4_ = bf16[128,896]{1,0:T(8,128)(2,1)S(1)} collective-permute-done((bf16[128,896]{1,0:T(8,128)(2,1)S(1)}, bf16[128,896]{1,0:T(8,128)(2,1)S(1)}, u32[]{:S(2)}, u32[]{:S(2)}) %collective-permute-start.3) | collective-permute-done | bytes 229408 | tf_op jit(solution)/shard_map/ppermute | solution.py:265
  205.7 12.3 %collective-permute-done.5.refs_6_ = bf16[128,896]{1,0:T(8,128)(2,1)S(1)} collective-permute-done((bf16[128,896]{1,0:T(8,128)(2,1)S(1)}, bf16[128,896]{1,0:T(8,128)(2,1)S(1)}, u32[]{:S(2)}, u32[]{:S(2)}) %collective-permute-start.5) | collective-permute-done | bytes 229408 | tf_op jit(solution)/shard_map/ppermute | solution.py:265
  218.0 9.5 %collective-permute-done.6.refs_7_ = bf16[128,896]{1,0:T(8,128)(2,1)S(1)} collective-permute-done((bf16[128,896]{1,0:T(8,128)(2,1)S(1)}, bf16[128,896]{1,0:T(8,128)(2,1)S(1)}, u32[]{:S(2)}, u32[]{:S(2)}) %collective-permute-start.6) | collective-permute-done | bytes 229408 | tf_op jit(solution)/shard_map/ppermute | solution.py:265
  227.5 7.6 %all-gather.6.cloned.1.call-done = bf16[4096,256]{1,0:T(8,128)(2,1)} async-done(((bf16[512,256]{1,0:T(8,128)(2,1)}), bf16[4096,256]{1,0:T(8,128)(2,1)}) %all-gather.6.cloned.1.call-update) | async-done | bytes 2097168 | tf_op jit(solution)/shard_map/all_gather | solution.py:278
  235.2 4.4 %expert_outputs.1 = bf16[256,896]{1,0:T(8,128)(2,1)} custom-call(s32[1]{0:T(128)} %bitcast.rank_ref, bf16[8,512,256]{2,1,0:T(8,128)(2,1)} %bitcast.11, bf16[128,896]{1,0:T(8,128)(2,1)} %get-tuple-element.34.refs_0_, bf16[128,896]{1,0:T(8,128)(2,1)} %copy-done.1, bf16[128,896]{1,0:T(8,128)(2,1)} %copy-done.2, bf16[128,896]{1,0:T(8,128)(2,1)} %copy-done.3, ...), custom_call_target="tpu_custom_call" | custom-call | tf_op jit(solution)/shard_map/expert_outputs/pallas_call | solution.py:196
  239.5 1.1 reshape.31
  240.7 48.3 %all_to_all.16 = bf16[64,4,896]{2,1,0:T(4,128)(2,1)S(1)} all-to-all(bf16[64,4,896]{2,1,0:T(4,128)(2,1)S(1)} %reshape.31), channel_id=1, replica_groups=mesh['expert'=64,'tensor'=8,'dp'=2] {'expert'}, dimensions={0} | all-to-all | bytes 917504 | tf_op jit(solution)/shard_map/all_to_all | solution.py:280
  289.8 2.2 combine.1
  (43 shorter events, 4.7 us)
Async XLA Ops:
  11.1 24.7 %all-to-all-start = ((bf16[16,32,896]{2,1,0:T(8,128)(2,1)}), bf16[16,32,896]{2,1,0:T(8,128)(2,1)S(1)}, u32[]{:S(2)}, u32[]{:S(2)}) async-start(bf16[16,32,896]{2,1,0:T(8,128)(2,1)} %bitcast.9), calls=%async_computation | async-start | bytes 1835008 | tf_op jit(solution)/shard_map/all_to_all | solution.py:250
  19.8 128.2 %all-gather.4.cloned.1.call-start = ((), (), s32[]{:S(2)}) async-start(), calls=%async_computation.3 | async-start | bytes 4128768 | tf_op jit(solution)/shard_map/all_gather | solution.py:270
  36.8 68.5 %copy-start.8 = (f32[3584]{0:T(1024)S(1)}, f32[3584]{0:T(1024)}, u32[]{:S(2)}) copy-start(f32[3584]{0:T(1024)} %param.12) | copy-start | bytes 43012
  105.2 129.9 %all-gather.6.cloned.1.call-start = ((), (), s32[]{:S(2)}) async-start(), calls=%async_computation.4 | async-start | bytes 2359296 | tf_op jit(solution)/shard_map/all_gather | solution.py:278
  148.0 8.8 %copy-start.15 = (bf16[128,896]{1,0:T(8,128)(2,1)S(1)}, bf16[128,896]{1,0:T(8,128)(2,1)}, u32[]{:S(2)}) copy-start(bf16[128,896]{1,0:T(8,128)(2,1)} %get-tuple-element.35) | copy-start | bytes 688132
  148.0 10.8 %copy-start.14 = (bf16[128,896]{1,0:T(8,128)(2,1)S(1)}, bf16[128,896]{1,0:T(8,128)(2,1)}, u32[]{:S(2)}) copy-start(bf16[128,896]{1,0:T(8,128)(2,1)} %get-tuple-element.36) | copy-start | bytes 688132
  148.0 15.8 %copy-start.13 = (bf16[128,896]{1,0:T(8,128)(2,1)S(1)}, bf16[128,896]{1,0:T(8,128)(2,1)}, u32[]{:S(2)}) copy-start(bf16[128,896]{1,0:T(8,128)(2,1)} %get-tuple-element.37) | copy-start | bytes 688132
  148.0 19.0 %copy-start.12 = (bf16[128,896]{1,0:T(8,128)(2,1)S(1)}, bf16[128,896]{1,0:T(8,128)(2,1)}, u32[]{:S(2)}) copy-start(bf16[128,896]{1,0:T(8,128)(2,1)} %get-tuple-element.38) | copy-start | bytes 688132
  148.0 23.2 %copy-start.11 = (bf16[128,896]{1,0:T(8,128)(2,1)S(1)}, bf16[128,896]{1,0:T(8,128)(2,1)}, u32[]{:S(2)}) copy-start(bf16[128,896]{1,0:T(8,128)(2,1)} %get-tuple-element.39) | copy-start | bytes 688132
  148.0 27.4 %copy-start.10 = (bf16[128,896]{1,0:T(8,128)(2,1)S(1)}, bf16[128,896]{1,0:T(8,128)(2,1)}, u32[]{:S(2)}) copy-start(bf16[128,896]{1,0:T(8,128)(2,1)} %get-tuple-element.40) | copy-start | bytes 688132
  148.0 32.5 %copy-start.9 = (bf16[128,896]{1,0:T(8,128)(2,1)S(1)}, bf16[128,896]{1,0:T(8,128)(2,1)}, u32[]{:S(2)}) copy-start(bf16[128,896]{1,0:T(8,128)(2,1)} %get-tuple-element.41) | copy-start | bytes 688132
  156.8 18.5 %collective-permute-start = (bf16[128,896]{1,0:T(8,128)(2,1)S(1)}, bf16[128,896]{1,0:T(8,128)(2,1)S(1)}, u32[]{:S(2)}, u32[]{:S(2)}) collective-permute-start(bf16[128,896]{1,0:T(8,128)(2,1)S(1)} %copy-done.15), channel_id=1, source_target_pairs={{0,2},{2,4},{4,6},{6,8},{8,10},{10,12},{12,14},{14,0},{1,3},{3,5},... | collective-permute-start | bytes 688136 | tf_op jit(solution)/shard_map/ppermute | solution.py:265
  158.8 21.8 %collective-permute-start.1 = (bf16[128,896]{1,0:T(8,128)(2,1)S(1)}, bf16[128,896]{1,0:T(8,128)(2,1)S(1)}, u32[]{:S(2)}, u32[]{:S(2)}) collective-permute-start(bf16[128,896]{1,0:T(8,128)(2,1)S(1)} %copy-done.14), channel_id=1, source_target_pairs={{0,4},{2,6},{4,8},{6,10},{8,12},{10,14},{12,0},{14,2},{1,5},{3,7},... | collective-permute-start | bytes 688136 | tf_op jit(solution)/shard_map/ppermute | solution.py:265
  163.8 28.7 %collective-permute-start.2 = (bf16[128,896]{1,0:T(8,128)(2,1)S(1)}, bf16[128,896]{1,0:T(8,128)(2,1)S(1)}, u32[]{:S(2)}, u32[]{:S(2)}) collective-permute-start(bf16[128,896]{1,0:T(8,128)(2,1)S(1)} %copy-done.13), channel_id=1, source_target_pairs={{0,6},{2,8},{4,10},{6,12},{8,14},{10,0},{12,2},{14,4},{1,7},{3,9},... | collective-permute-start | bytes 688136 | tf_op jit(solution)/shard_map/ppermute | solution.py:265
  167.0 38.7 %collective-permute-start.3 = (bf16[128,896]{1,0:T(8,128)(2,1)S(1)}, bf16[128,896]{1,0:T(8,128)(2,1)S(1)}, u32[]{:S(2)}, u32[]{:S(2)}) collective-permute-start(bf16[128,896]{1,0:T(8,128)(2,1)S(1)} %copy-done.12), channel_id=1, source_target_pairs={{0,8},{2,10},{4,12},{6,14},{8,0},{10,2},{12,4},{14,6},{1,9},{3,11}... | collective-permute-start | bytes 688136 | tf_op jit(solution)/shard_map/ppermute | solution.py:265
  171.2 34.5 %collective-permute-start.4 = (bf16[128,896]{1,0:T(8,128)(2,1)S(1)}, bf16[128,896]{1,0:T(8,128)(2,1)S(1)}, u32[]{:S(2)}, u32[]{:S(2)}) collective-permute-start(bf16[128,896]{1,0:T(8,128)(2,1)S(1)} %copy-done.11), channel_id=1, source_target_pairs={{0,10},{2,12},{4,14},{6,0},{8,2},{10,4},{12,6},{14,8},{1,11},{3,13... | collective-permute-start | bytes 688136 | tf_op jit(solution)/shard_map/ppermute | solution.py:265
  175.4 59.8 %copy-start.1 = (bf16[128,896]{1,0:T(8,128)(2,1)}, bf16[128,896]{1,0:T(8,128)(2,1)S(1)}, u32[]{:S(2)}) copy-start(bf16[128,896]{1,0:T(8,128)(2,1)S(1)} %collective-permute-done.refs_1_) | copy-start | bytes 688132
  175.4 42.6 %collective-permute-start.5 = (bf16[128,896]{1,0:T(8,128)(2,1)S(1)}, bf16[128,896]{1,0:T(8,128)(2,1)S(1)}, u32[]{:S(2)}, u32[]{:S(2)}) collective-permute-start(bf16[128,896]{1,0:T(8,128)(2,1)S(1)} %copy-done.10), channel_id=1, source_target_pairs={{0,12},{2,14},{4,0},{6,2},{8,4},{10,6},{12,8},{14,10},{1,13},{3,15... | collective-permute-start | bytes 688136 | tf_op jit(solution)/shard_map/ppermute | solution.py:265
  180.6 54.6 %copy-start.2 = (bf16[128,896]{1,0:T(8,128)(2,1)}, bf16[128,896]{1,0:T(8,128)(2,1)S(1)}, u32[]{:S(2)}) copy-start(bf16[128,896]{1,0:T(8,128)(2,1)S(1)} %collective-permute-done.1.refs_2_) | copy-start | bytes 688132
  180.6 47.0 %collective-permute-start.6 = (bf16[128,896]{1,0:T(8,128)(2,1)S(1)}, bf16[128,896]{1,0:T(8,128)(2,1)S(1)}, u32[]{:S(2)}, u32[]{:S(2)}) collective-permute-start(bf16[128,896]{1,0:T(8,128)(2,1)S(1)} %copy-done.9), channel_id=1, source_target_pairs={{0,14},{2,0},{4,2},{6,4},{8,6},{10,8},{12,10},{14,12},{1,15},{3,1}... | collective-permute-start | bytes 688136 | tf_op jit(solution)/shard_map/ppermute | solution.py:265
  192.5 42.6 %copy-start.3 = (bf16[128,896]{1,0:T(8,128)(2,1)}, bf16[128,896]{1,0:T(8,128)(2,1)S(1)}, u32[]{:S(2)}) copy-start(bf16[128,896]{1,0:T(8,128)(2,1)S(1)} %collective-permute-done.2.refs_3_) | copy-start | bytes 688132
  205.7 29.4 %copy-start.4 = (bf16[128,896]{1,0:T(8,128)(2,1)}, bf16[128,896]{1,0:T(8,128)(2,1)S(1)}, u32[]{:S(2)}) copy-start(bf16[128,896]{1,0:T(8,128)(2,1)S(1)} %collective-permute-done.3.refs_4_) | copy-start | bytes 688132
  205.7 29.4 %copy-start.5 = (bf16[128,896]{1,0:T(8,128)(2,1)}, bf16[128,896]{1,0:T(8,128)(2,1)S(1)}, u32[]{:S(2)}) copy-start(bf16[128,896]{1,0:T(8,128)(2,1)S(1)} %collective-permute-done.4.refs_5_) | copy-start | bytes 688132
  218.0 17.2 %copy-start.6 = (bf16[128,896]{1,0:T(8,128)(2,1)}, bf16[128,896]{1,0:T(8,128)(2,1)S(1)}, u32[]{:S(2)}) copy-start(bf16[128,896]{1,0:T(8,128)(2,1)S(1)} %collective-permute-done.5.refs_6_) | copy-start | bytes 688132
  (2 other events, 8.6 us)
Sparse Core Ops, SparseCore 0:
  105.4 42.5 all-gather.3
  156.9 78.1 all-gather.5

commit v3 on v1

v3 whole, which is shorter than its diff:
```python
import functools

import jax
import jax.numpy as jnp
from jax import lax
from jax.experimental import pallas as pl
from jax.experimental.pallas import tpu as pltpu
from jax.sharding import PartitionSpec as P

norm_eps = 1e-06
route_scale = 2.5
bf16 = jnp.bfloat16
f32 = jnp.float32


def mm(a, b, contract=(1, 0)):
    return lax.dot_general(
        a, b, (((contract[0],), (contract[1],)), ((), ())), preferred_element_type=f32
    )


def project_kernel(attn_ref, weight_ref, out_ref):
    own_half = out_ref.shape[2]
    part = out_ref.shape[3] // 2
    value = mm(attn_ref[...], weight_ref[...]).astype(bf16)
    for j in range(2):
        for d in range(out_ref.shape[1]):
            for h in range(2):
                row = (d * 2 + h) * own_half
                out_ref[j, d, :, h * part : (h + 1) * part] = value[
                    row : row + own_half, j * part : (j + 1) * part
                ]


def project(attn_out, out_weight, tensor_count, dp_count):
    rows, depth = attn_out.shape
    width = out_weight.shape[1]
    part = width // tensor_count
    own = rows // dp_count
    return pl.pallas_call(
        project_kernel,
        grid=(tensor_count // 2,),
        in_specs=[
            pl.BlockSpec((rows, depth), lambda s: (0, 0)),
            pl.BlockSpec((depth, 2 * part), lambda s: (0, s)),
        ],
        out_specs=pl.BlockSpec((2, dp_count, own // 2, 2 * part), lambda s: (s, 0, 0, 0)),
        out_shape=jax.ShapeDtypeStruct((tensor_count, dp_count, own // 2, 2 * part), bf16),
        name="project",
    )(attn_out, out_weight)


def slots_of(routes, experts):
    own = routes.shape[1]
    expert_row = lax.broadcasted_iota(jnp.int32, (experts, own), 0)
    named = jnp.zeros((experts, own), f32)
    for k in range(routes.shape[0]):
        named = named + jnp.where(routes[k : k + 1, :] == expert_row, 1.0, 0.0)
    before = jnp.where(
        lax.broadcasted_iota(jnp.int32, (own, own), 0)
        < lax.broadcasted_iota(jnp.int32, (own, own), 1),
        1.0,
        0.0,
    ).astype(bf16)
    return named, mm(named.astype(bf16), before), expert_row


def dispatch_kernel(parts_ref, residual_ref, routes_ref, stream_ref, *sent_refs):
    part = stream_ref.shape[1]
    total = parts_ref[0].astype(f32)
    for i in range(1, parts_ref.shape[0]):
        total = total + parts_ref[i].astype(f32)
    attn = jnp.concatenate([total[:, :part], total[:, part:]], axis=0)
    stream = (residual_ref[...].astype(f32) + attn).astype(bf16)
    stream_ref[...] = stream
    named, slot, _ = slots_of(routes_ref[...], sent_refs[0].shape[0])
    first = 0
    for sent_ref in sent_refs:
        for g in range(sent_ref.shape[1] // part):
            pick = jnp.where(slot == first, named, 0.0).astype(bf16)
            sent_ref[:, g * part : (g + 1) * part] = mm(pick, stream).astype(bf16)
            first += 1


def expert_kernel(steps, x_ref, gain_ref, gate_ref, up_ref, down_ref, out_ref, gate_acc, up_acc, square_acc, hidden):
    step = pl.program_id(0)
    slices, _, part = gain_ref.shape
    rows = x_ref.shape[1]
    segments = x_ref.shape[2] // part
    width = part * slices * steps
    lanes = square_acc.shape[1]

    @pl.when(step < steps)
    def _():
        gate = up = None
        square = [None] * segments
        for k in range(slices):
            scaled = []
            for g in range(segments):
                wide = x_ref[k, :, g * part : (g + 1) * part].astype(f32)
                scaled.append((wide * gain_ref[k]).astype(bf16))
                powers = wide * wide
                for c in range(0, part, lanes):
                    piece = powers[:, c : c + lanes]
                    if piece.shape[1] < lanes:
                        piece = jnp.concatenate(
                            [piece, jnp.zeros((rows, lanes - piece.shape[1]), f32)], axis=1
                        )
                    square[g] = piece if square[g] is None else square[g] + piece
            scaled = jnp.concatenate(scaled, axis=0)
            depth = slice(k * part, (k + 1) * part)
            gate_term = mm(scaled, gate_ref[depth, :])
            up_term = mm(scaled, up_ref[depth, :])
            gate = gate_term if gate is None else gate + gate_term
            up = up_term if up is None else up + up_term
        square = jnp.concatenate(square, axis=0)

        @pl.when(step == 0)
        def _():
            gate_acc[...] = gate
            up_acc[...] = up
            square_acc[...] = square

        @pl.when(step > 0)
        def _():
            gate_acc[...] += gate
            up_acc[...] += up
            square_acc[...] += square

    @pl.when(step == steps - 1)
    def _():
        mean = jnp.sum(square_acc[...], axis=1, keepdims=True) / width
        inverse = lax.rsqrt(mean + norm_eps)
        gate = inverse * gate_acc[...]
        up = inverse * up_acc[...]
        hidden[...] = (jax.nn.silu(gate) * up).astype(bf16)

    @pl.when(step >= steps)
    def _():
        for j in range(0, out_ref.shape[0], 2):
            term = mm(hidden[...], down_ref[:, j * part : (j + 2) * part]).astype(bf16)
            for g in range(segments):
                for i in range(2):
                    out_ref[j + i, :, g * part : (g + 1) * part] = term[
                        g * rows : (g + 1) * rows, i * part : (i + 1) * part
                    ]


def expert_layer(x, gain, gate_weights, up_weights, down_weights):
    count, rows, wide = x.shape
    width, hidden_width = gate_weights.shape
    part = width // count
    total_rows = rows * (wide // part)
    slices, outs = 2, 4
    steps = count // slices

    def late(s):
        return jnp.maximum(s - steps, 0)

    return pl.pallas_call(
        functools.partial(expert_kernel, steps),
        grid=(steps + count // outs,),
        in_specs=[
            pl.BlockSpec((slices, rows, wide), lambda s: (jnp.minimum(s, steps - 1), 0, 0)),
            pl.BlockSpec((slices, 1, part), lambda s: (jnp.minimum(s, steps - 1), 0, 0)),
            pl.BlockSpec((slices * part, hidden_width), lambda s: (jnp.minimum(s, steps - 1), 0)),
            pl.BlockSpec((slices * part, hidden_width), lambda s: (jnp.minimum(s, steps - 1), 0)),
            pl.BlockSpec((hidden_width, outs * part), lambda s: (0, late(s))),
        ],
        out_specs=pl.BlockSpec((outs, rows, wide), lambda s: (late(s), 0, 0)),
        out_shape=jax.ShapeDtypeStruct((count, rows, wide), bf16),
        scratch_shapes=[
            pltpu.VMEM((total_rows, hidden_width), f32),
            pltpu.VMEM((total_rows, hidden_width), f32),
            pltpu.VMEM((total_rows, 128), f32),
            pltpu.VMEM((total_rows, hidden_width), bf16),
        ],
        name="expert_layer",
    )(x, gain.reshape(count, 1, part), gate_weights, up_weights, down_weights)


def combine_kernel(stream_ref, routes_ref, values_ref, *refs):
    returned_refs, out_ref = refs[:-1], refs[-1]
    part = stream_ref.shape[1]
    routes = routes_ref[...]
    values = values_ref[...].astype(f32)
    mix = (route_scale * values / jnp.sum(values, axis=0, keepdims=True)).astype(bf16).astype(f32)
    _, slot, expert_row = slots_of(routes, returned_refs[0].shape[0])
    weight = jnp.zeros(expert_row.shape, f32)
    for k in range(routes.shape[0]):
        weight = weight + jnp.where(routes[k : k + 1, :] == expert_row, mix[k : k + 1, :], 0.0)
    moe = stream_ref[...].astype(f32)
    first = 0
    for returned_ref in returned_refs:
        for g in range(returned_ref.shape[1] // part):
            pick = jnp.where(slot == first, weight, 0.0).astype(bf16)
            moe = moe + mm(pick, returned_ref[:, g * part : (g + 1) * part], (0, 0))
            first += 1
    out_ref[...] = moe.astype(bf16)


def swap(x, axis):
    return lax.all_to_all(x, axis, split_axis=0, concat_axis=0, tiled=True)


def body(
    attn_out,
    out_weight,
    residual,
    norm_gain,
    gate_weights,
    up_weights,
    down_weights,
    routes,
    gate_values,
):
    tensor_count = lax.axis_size("tensor")
    dp_count = lax.axis_size("dp")
    expert_count = lax.axis_size("expert")
    own_tokens = attn_out.shape[0] // dp_count
    part = out_weight.shape[1] // tensor_count
    capacity = own_tokens * routes.shape[1] // expert_count
    few = capacity // 4
    wide_a, wide_b = (capacity - few) * part, few * part
    weights = (norm_gain, gate_weights[0], up_weights[0], down_weights[0])

    def to_experts(sent):
        pairs = sent.reshape(expert_count, 2, sent.shape[1] // 2)
        return swap(pairs, "expert").reshape(sent.shape)

    parts = project(attn_out, out_weight, tensor_count, dp_count)
    parts = swap(parts.reshape(tensor_count * dp_count, own_tokens // 2, 2 * part), ("tensor", "dp"))
    stream, sent_a, sent_b = pl.pallas_call(
        dispatch_kernel,
        out_shape=(
            jax.ShapeDtypeStruct((own_tokens, part), bf16),
            jax.ShapeDtypeStruct((expert_count, wide_a), bf16),
            jax.ShapeDtypeStruct((expert_count, wide_b), bf16),
        ),
        name="dispatch",
    )(parts, residual, routes.T)

    rows_a = to_experts(sent_a)
    rows_a, sent_b = lax.optimization_barrier((rows_a, sent_b))
    whole_a = lax.all_gather(rows_a, "tensor", axis=0, tiled=False)
    rows_b = to_experts(sent_b)
    copies_b = lax.optimization_barrier(
        jnp.broadcast_to(rows_b[None], (tensor_count, *rows_b.shape))
    )
    whole_b = swap(copies_b, "tensor")
    whole_a, whole_b = lax.optimization_barrier((whole_a, whole_b))

    term_a = expert_layer(whole_a, *weights)
    term_a, whole_b = lax.optimization_barrier((term_a, whole_b))
    summed_a = lax.psum_scatter(term_a, "tensor", scatter_dimension=0, tiled=False)
    term_b = swap(expert_layer(whole_b, *weights), "tensor")
    summed_b = jnp.sum(term_b.astype(f32), axis=0).astype(bf16)
    returned_b = to_experts(summed_b)
    summed_a, returned_b = lax.optimization_barrier((summed_a, returned_b))
    returned_a = to_experts(summed_a)
    return pl.pallas_call(
        combine_kernel,
        out_shape=jax.ShapeDtypeStruct((own_tokens, part), bf16),
        name="combine",
    )(stream, routes.T, gate_values.T, returned_a, returned_b)


def solution(mesh):
    return jax.shard_map(
        body,
        mesh=mesh,
        in_specs=(
            P("expert", ("tensor", "dp")),
            P(("tensor", "dp"), None),
            P(("expert", "dp"), "tensor"),
            P(),
            P("expert", None, "tensor"),
            P("expert", None, "tensor"),
            P("expert", "tensor", None),
            P(("expert", "dp"), None),
            P(("expert", "dp"), None),
        ),
        out_specs=P(("expert", "dp"), "tensor"),
        check_vma=False,
    )
```

time: 277 us -> 288 us (1.040)
  waiting for transfers between devices: 99.2 us -> 25.8 us
  blocking collectives: 137 us -> 210 us
  local copies, waits for them, and re-layouts: 4.7 us -> 8.58 us
  Pallas kernels: 22 us -> 25.7 us
  starting transfers between devices: 0.04 us -> 3.6 us
    all_to_all x3 -> x6, blocking collectives: 137 us -> 210 us  [swap(): return lax.all_to_all(x, axis, split_axis=0, concat_axis=0, tiled=True)]
    reduce_scatter x1, waiting for transfers between devices: 56.9 us -> 0.01 us  [body(): lax.psum_scatter(term_a, 'tensor', scatter_dimension=0, tiled=False)]
    all_gather x1, waiting for transfers between devices: 42.2 us -> 0.01 us  [body(): whole_a = lax.all_gather(rows_a, 'tensor', axis=0, tiled=False)]
    all_to_all x0 -> x1, waiting for transfers between devices: none -> 25.7 us  [swap(): return lax.all_to_all(x, axis, split_axis=0, concat_axis=0, tiled=True)]
    pallas_call x3 -> x4, Pallas kernels: 17.4 us -> 21.2 us  [the longest x2 16.4 us: expert_layer(): pl.pallas_call(functools.partial(expert_kernel, steps), grid=(steps + cou...]
    all_to_all x0 -> x1, starting transfers between devices: none -> 3.55 us  [swap(): return lax.all_to_all(x, axis, split_axis=0, concat_axis=0, tiled=True)]
    reshape x5 -> x8, local copies, waits for them, and re-layouts: 4.69 us -> 7.39 us  [the longest x4 3.91 us: to_experts(): pairs = sent.reshape(expert_count, 2, sent.shape[1] // 2)]
  transfers between devices with their start and end apart: 2 -> 3, of which waited for: 2 -> 1; matrix products, arithmetic and copies ran while one was open for 0% -> 1% of each run, Pallas kernels for 0% -> 2%
where the time goes in v3:
time: 288 us; the launch traced here: 287 us
  blocking collectives  210 us (73%)
  waiting for transfers between devices  25.8 us (9%)
  Pallas kernels  25.7 us (9%)
  between operations  13.5 us (5%)
  local copies, waits for them, and re-layouts  8.58 us (3%)
  starting transfers between devices  3.6 us (1%)
    all_to_all x6, blocking collectives, swap(): return lax.all_to_all(x, axis, split_axis=0, concat_axis=0, tiled=True)  210 us
    all_to_all x1, waiting for transfers between devices, swap(): return lax.all_to_all(x, axis, split_axis=0, concat_axis=0, tiled=True)  25.7 us
    pallas_call x2, Pallas kernels, expert_layer(): pl.pallas_call(functools.partial(expert_kernel, steps), grid=(steps + cou...  16.4 us
  transfers between devices with their start and end apart: 3, of which 1 were waited for; matrix products, arithmetic and copies ran while one was open for 1% of the time, Pallas kernels for 2%

profile of v3, /device:TPU:1, one launch (start us, length us, event | category | flops | bytes accessed | tf_op | source)
XLA Modules:
  0.0 286.9 jit_solution(4315368893848347042)
XLA Ops:
  6.5 4.6 %project.1 = bf16[8,2,32,896]{3,2,1,0:T(8,128)(2,1)} custom-call(bf16[128,512]{1,0:T(8,128)(2,1)} %attn_ref.1, bf16[512,3584]{1,0:T(8,128)(2,1)} %weight_ref.1), custom_call_target="tpu_custom_call" | custom-call | tf_op jit(solution)/shard_map/project/pallas_call | solution.py:40
  11.1 25.2 %all_to_all.35.parts_ref = bf16[16,32,896]{2,1,0:T(8,128)(2,1)} all-to-all(bf16[16,32,896]{2,1,0:T(8,128)(2,1)} %bitcast.14), channel_id=1, replica_groups=mesh['expert'=64,'tensor'=8,'dp'=2] {'tensor','dp'}, dimensions={0} | all-to-all | bytes 1835008 | tf_op jit(solution)/shard_map/all_to_all | solution.py:203
  36.4 2.5 dispatch.1
  38.9 1.3 reshape.30
  40.2 59.4 %all_to_all.36 = bf16[64,2,1344]{2,1,0:T(2,128)(2,1)S(1)} all-to-all(bf16[64,2,1344]{2,1,0:T(2,128)(2,1)S(1)} %reshape.30), channel_id=1, replica_groups=mesh['expert'=64,'tensor'=8,'dp'=2] {'expert'}, dimensions={0} | all-to-all | bytes 688128 | tf_op jit(solution)/shard_map/all_to_all | solution.py:203
  99.6 1.0 reshape.31
  100.6 1.1 reshape.32
  101.7 22.3 %all_to_all.37 = bf16[64,2,448]{2,1,0:T(2,128)(2,1)S(1)} all-to-all(bf16[64,2,448]{2,1,0:T(2,128)(2,1)S(1)} %reshape.32), channel_id=1, replica_groups=mesh['expert'=64,'tensor'=8,'dp'=2] {'expert'}, dimensions={0} | all-to-all | bytes 229376 | tf_op jit(solution)/shard_map/all_to_all | solution.py:203
  124.0 0.1 broadcast_in_dim.7
  124.1 1.0 broadcast_in_dim.8
  125.2 3.6 %all-to-all-start.3 = ((bf16[8,64,896]{2,1,0:T(8,128)(2,1)}), bf16[8,64,896]{2,1,0:T(8,128)(2,1)S(1)}, u32[]{:S(2)}, u32[]{:S(2)}) async-start(bf16[8,64,896]{2,1,0:T(8,128)(2,1)} %broadcast_in_dim.8), calls=%async_computation.3 | async-start | bytes 1835008 | tf_op jit(solution)/shard_map/all_to_all | solution.py:203
  128.8 0.7 reshape.33.gain_ref
  129.5 25.7 %all-to-all-done.3.x_ref = bf16[8,64,896]{2,1,0:T(8,128)(2,1)S(1)} async-done(((bf16[8,64,896]{2,1,0:T(8,128)(2,1)}), bf16[8,64,896]{2,1,0:T(8,128)(2,1)S(1)}, u32[]{:S(2)}, u32[]{:S(2)}) %all-to-all-start.3) | async-done | bytes 917536 | tf_op jit(solution)/shard_map/all_to_all | solution.py:203
  155.2 9.5 %expert_layer.2 = bf16[8,64,2688]{2,1,0:T(8,128)(2,1)} custom-call(bf16[8,64,2688]{2,1,0:T(8,128)(2,1)} %bitcast.15, f32[8,1,448]{2,1,0:T(1,128)} %reshape.33.gain_ref, bf16[3584,256]{1,0:T(8,128)(2,1)} %bitcast.8, bf16[3584,256]{1,0:T(8,128)(2,1)} %bitcast.10, bf16[256,3584]{1,0:T(8,128)(2,1)} %bitcast.12), custom_call_target="tpu_custom_call" | custom-call | tf_op jit(solution)/shard_map/expert_layer/pallas_call | solution.py:160
  164.8 6.9 %expert_layer.3 = bf16[8,64,896]{2,1,0:T(8,128)(2,1)} custom-call(bf16[8,64,896]{2,1,0:T(8,128)(2,1)} %copy-done, f32[8,1,448]{2,1,0:T(1,128)} %reshape.33.gain_ref, bf16[3584,256]{1,0:T(8,128)(2,1)} %bitcast.9, bf16[3584,256]{1,0:T(8,128)(2,1)} %bitcast.11, bf16[256,3584]{1,0:T(8,128)(2,1)} %bitcast.13), custom_call_target="tpu_custom_call" | custom-call | tf_op jit(solution)/shard_map/expert_layer/pallas_call | solution.py:160
  171.7 34.1 %all_to_all.38 = bf16[8,64,896]{2,1,0:T(8,128)(2,1)S(1)} all-to-all(bf16[8,64,896]{2,1,0:T(8,128)(2,1)} %expert_layer.3), channel_id=1, replica_groups=mesh['expert'=64,'tensor'=8,'dp'=2] {'tensor'}, dimensions={0} | all-to-all | bytes 1835008 | tf_op jit(solution)/shard_map/all_to_all | solution.py:203
  205.8 0.1 reduce_sum.12
  206.0 0.2 reshape.34
  206.1 36.9 %all_to_all.39 = bf16[64,2,448]{2,1,0:T(2,128)(2,1)S(1)} all-to-all(bf16[64,2,448]{2,1,0:T(2,128)(2,1)S(1)} %reshape.34), channel_id=1, replica_groups=mesh['expert'=64,'tensor'=8,'dp'=2] {'expert'}, dimensions={0} | all-to-all | bytes 229376 | tf_op jit(solution)/shard_map/all_to_all | solution.py:203
  243.0 0.8 reshape.35.refs_1_
  243.8 1.3 reshape.36
  245.2 31.7 %all_to_all.40 = bf16[64,2,1344]{2,1,0:T(2,128)(2,1)S(1)} all-to-all(bf16[64,2,1344]{2,1,0:T(2,128)(2,1)S(1)} %reshape.36), channel_id=1, replica_groups=mesh['expert'=64,'tensor'=8,'dp'=2] {'expert'}, dimensions={0} | all-to-all | bytes 688128 | tf_op jit(solution)/shard_map/all_to_all | solution.py:203
  276.9 1.0 reshape.37.refs_0_
  277.9 2.2 combine.1
  (10 shorter events, 0.1 us)
Async XLA Ops:
  6.5 148.7 %all-gather.3.cloned.1.call-start = ((), (), s32[]{:S(2)}) async-start(), calls=%async_computation.9 | async-start | bytes 3096576 | tf_op jit(solution)/shard_map/all_gather | solution.py:245
  40.2 88.6 %copy-start.1 = (f32[3584]{0:T(1024)S(1)}, f32[3584]{0:T(1024)}, u32[]{:S(2)}) copy-start(f32[3584]{0:T(1024)} %param.12) | copy-start | bytes 43012
  125.2 30.0 %all-to-all-start.3 = ((bf16[8,64,896]{2,1,0:T(8,128)(2,1)}), bf16[8,64,896]{2,1,0:T(8,128)(2,1)S(1)}, u32[]{:S(2)}, u32[]{:S(2)}) async-start(bf16[8,64,896]{2,1,0:T(8,128)(2,1)} %broadcast_in_dim.8), calls=%async_computation.3 | async-start | bytes 1835008 | tf_op jit(solution)/shard_map/all_to_all | solution.py:203
  128.8 115.1 %reduce-scatter.2.cloned.1.call-start = ((), (), s32[]{:S(2)}) async-start(), calls=%async_computation.8 | async-start | bytes 3096576 | tf_op jit(solution)/shard_map/reduce_scatter | solution.py:255
  155.2 9.5 %copy-start = (bf16[8,64,896]{2,1,0:T(8,128)(2,1)}, bf16[8,64,896]{2,1,0:T(8,128)(2,1)S(1)}, u32[]{:S(2)}) copy-start(bf16[8,64,896]{2,1,0:T(8,128)(2,1)S(1)} %all-to-all-done.3.x_ref) | copy-start | bytes 2752516
Sparse Core Ops, SparseCore 0:
  100.7 34.3 all-gather.2
  164.9 60.1 reduce-scatter.1

commit v4 on v3

--- a/solution.py
+++ b/solution.py
@@ -46,8 +46,9 @@
         ],
         out_specs=pl.BlockSpec((2, dp_count, own // 2, 2 * part), lambda s: (s, 0, 0, 0)),
         out_shape=jax.ShapeDtypeStruct((tensor_count, dp_count, own // 2, 2 * part), bf16),
+        compiler_params=pltpu.CompilerParams(vmem_limit_bytes=16 << 20),
         name="project",
-    )(attn_out, out_weight)
+    )(attn_out, in_hbm(out_weight))
 
 
 def slots_of(routes, experts):
@@ -65,7 +66,7 @@
     return named, mm(named.astype(bf16), before), expert_row
 
 
-def dispatch_kernel(parts_ref, residual_ref, routes_ref, stream_ref, *sent_refs):
+def dispatch_kernel(parts_ref, residual_ref, routes_ref, stream_ref, sent_ref):
     part = stream_ref.shape[1]
     total = parts_ref[0].astype(f32)
     for i in range(1, parts_ref.shape[0]):
@@ -73,13 +74,14 @@
     attn = jnp.concatenate([total[:, :part], total[:, part:]], axis=0)
     stream = (residual_ref[...].astype(f32) + attn).astype(bf16)
     stream_ref[...] = stream
-    named, slot, _ = slots_of(routes_ref[...], sent_refs[0].shape[0])
-    first = 0
-    for sent_ref in sent_refs:
-        for g in range(sent_ref.shape[1] // part):
-            pick = jnp.where(slot == first, named, 0.0).astype(bf16)
-            sent_ref[:, g * part : (g + 1) * part] = mm(pick, stream).astype(bf16)
-            first += 1
+    named, slot, _ = slots_of(routes_ref[...], sent_ref.shape[0])
+    segments = sent_ref.shape[2] // part
+    for g in range(segments):
+        lines = []
+        for i in range(2):
+            pick = jnp.where(slot == i * segments + g, named, 0.0).astype(bf16)
+            lines.append(mm(pick, stream)[:, None, :])
+        sent_ref[:, :, g * part : (g + 1) * part] = jnp.concatenate(lines, axis=1).astype(bf16)
 
 
 def expert_kernel(steps, x_ref, gain_ref, gate_ref, up_ref, down_ref, out_ref, gate_acc, up_acc, square_acc, hidden):
@@ -109,7 +111,8 @@
                     square[g] = piece if square[g] is None else square[g] + piece
             scaled = jnp.concatenate(scaled, axis=0)
             depth = slice(k * part, (k + 1) * part)
-            gate_term = mm(scaled, gate_ref[depth, :])
+            whole_depth = pl.ds(pl.multiple_of((step * slices + k) * part, 64), part)
+            gate_term = mm(scaled, gate_ref[whole_depth, :])
             up_term = mm(scaled, up_ref[depth, :])
             gate = gate_term if gate is None else gate + gate_term
             up = up_term if up is None else up + up_term
@@ -163,40 +166,44 @@
         in_specs=[
             pl.BlockSpec((slices, rows, wide), lambda s: (jnp.minimum(s, steps - 1), 0, 0)),
             pl.BlockSpec((slices, 1, part), lambda s: (jnp.minimum(s, steps - 1), 0, 0)),
-            pl.BlockSpec((slices * part, hidden_width), lambda s: (jnp.minimum(s, steps - 1), 0)),
+            pl.BlockSpec(memory_space=pltpu.VMEM),
             pl.BlockSpec((slices * part, hidden_width), lambda s: (jnp.minimum(s, steps - 1), 0)),
             pl.BlockSpec((hidden_width, outs * part), lambda s: (0, late(s))),
         ],
         out_specs=pl.BlockSpec((outs, rows, wide), lambda s: (late(s), 0, 0)),
-        out_shape=jax.ShapeDtypeStruct((count, rows, wide), bf16),
+        out_shape=pltpu.HBM((count, rows, wide), bf16),
         scratch_shapes=[
             pltpu.VMEM((total_rows, hidden_width), f32),
             pltpu.VMEM((total_rows, hidden_width), f32),
             pltpu.VMEM((total_rows, 128), f32),
             pltpu.VMEM((total_rows, hidden_width), bf16),
         ],
+        compiler_params=pltpu.CompilerParams(vmem_limit_bytes=28 << 20),
         name="expert_layer",
     )(x, gain.reshape(count, 1, part), gate_weights, up_weights, down_weights)
 
 
-def combine_kernel(stream_ref, routes_ref, values_ref, *refs):
-    returned_refs, out_ref = refs[:-1], refs[-1]
+def combine_kernel(stream_ref, routes_ref, values_ref, returned_ref, out_ref):
     part = stream_ref.shape[1]
     routes = routes_ref[...]
     values = values_ref[...].astype(f32)
     mix = (route_scale * values / jnp.sum(values, axis=0, keepdims=True)).astype(bf16).astype(f32)
-    _, slot, expert_row = slots_of(routes, returned_refs[0].shape[0])
+    _, slot, expert_row = slots_of(routes, returned_ref.shape[0])
     weight = jnp.zeros(expert_row.shape, f32)
     for k in range(routes.shape[0]):
         weight = weight + jnp.where(routes[k : k + 1, :] == expert_row, mix[k : k + 1, :], 0.0)
     moe = stream_ref[...].astype(f32)
-    first = 0
-    for returned_ref in returned_refs:
-        for g in range(returned_ref.shape[1] // part):
-            pick = jnp.where(slot == first, weight, 0.0).astype(bf16)
-            moe = moe + mm(pick, returned_ref[:, g * part : (g + 1) * part], (0, 0))
-            first += 1
+    segments = returned_ref.shape[2] // part
+    for g in range(segments):
+        pair = returned_ref[:, :, g * part : (g + 1) * part].astype(f32)
+        for i in range(2):
+            pick = jnp.where(slot == i * segments + g, weight, 0.0).astype(bf16)
+            moe = moe + mm(pick, pair[:, i, :].astype(bf16), (0, 0))
     out_ref[...] = moe.astype(bf16)
+
+
+def in_hbm(x):
+    return pltpu.with_memory_space_constraint(x, pltpu.HBM)
 
 
 def swap(x, axis):
@@ -220,49 +227,36 @@
     own_tokens = attn_out.shape[0] // dp_count
     part = out_weight.shape[1] // tensor_count
     capacity = own_tokens * routes.shape[1] // expert_count
-    few = capacity // 4
-    wide_a, wide_b = (capacity - few) * part, few * part
-    weights = (norm_gain, gate_weights[0], up_weights[0], down_weights[0])
-
-    def to_experts(sent):
-        pairs = sent.reshape(expert_count, 2, sent.shape[1] // 2)
-        return swap(pairs, "expert").reshape(sent.shape)
 
     parts = project(attn_out, out_weight, tensor_count, dp_count)
     parts = swap(parts.reshape(tensor_count * dp_count, own_tokens // 2, 2 * part), ("tensor", "dp"))
-    stream, sent_a, sent_b = pl.pallas_call(
+    stream, sent = pl.pallas_call(
         dispatch_kernel,
         out_shape=(
             jax.ShapeDtypeStruct((own_tokens, part), bf16),
-            jax.ShapeDtypeStruct((expert_count, wide_a), bf16),
-            jax.ShapeDtypeStruct((expert_count, wide_b), bf16),
+            jax.ShapeDtypeStruct((expert_count, 2, capacity // 2 * part), bf16),
         ),
+        compiler_params=pltpu.CompilerParams(vmem_limit_bytes=16 << 20),
         name="dispatch",
     )(parts, residual, routes.T)
 
-    rows_a = to_experts(sent_a)
-    rows_a, sent_b = lax.optimization_barrier((rows_a, sent_b))
-    whole_a = lax.all_gather(rows_a, "tensor", axis=0, tiled=False)
-    rows_b = to_experts(sent_b)
-    copies_b = lax.optimization_barrier(
-        jnp.broadcast_to(rows_b[None], (tensor_count, *rows_b.shape))
+    whole = lax.all_gather(
+        swap(sent, "expert").reshape(expert_count, capacity * part), "tensor", axis=0, tiled=False)
+    term = expert_layer(
+        in_hbm(whole),
+        norm_gain,
+        pltpu.with_memory_space_constraint(gate_weights[0], pltpu.VMEM),
+        in_hbm(up_weights[0]),
+        in_hbm(down_weights[0]),
     )
-    whole_b = swap(copies_b, "tensor")
-    whole_a, whole_b = lax.optimization_barrier((whole_a, whole_b))
-
-    term_a = expert_layer(whole_a, *weights)
-    term_a, whole_b = lax.optimization_barrier((term_a, whole_b))
-    summed_a = lax.psum_scatter(term_a, "tensor", scatter_dimension=0, tiled=False)
-    term_b = swap(expert_layer(whole_b, *weights), "tensor")
-    summed_b = jnp.sum(term_b.astype(f32), axis=0).astype(bf16)
-    returned_b = to_experts(summed_b)
-    summed_a, returned_b = lax.optimization_barrier((summed_a, returned_b))
-    returned_a = to_experts(summed_a)
+    summed = lax.psum_scatter(term, "tensor", scatter_dimension=0, tiled=False)
+    returned = swap(summed.reshape(expert_count, 2, capacity // 2 * part), "expert")
     return pl.pallas_call(
         combine_kernel,
         out_shape=jax.ShapeDtypeStruct((own_tokens, part), bf16),
+        compiler_params=pltpu.CompilerParams(vmem_limit_bytes=16 << 20),
         name="combine",
-    )(stream, routes.T, gate_values.T, returned_a, returned_b)
+    )(stream, routes.T, gate_values.T, returned)
 
 
 def solution(mesh):

time: 288 us -> 271 us (0.941)
  waiting for transfers between devices: 25.8 us -> 99.8 us
  blocking collectives: 210 us -> 137 us
  Pallas kernels: 25.7 us -> 17.2 us
  local copies, waits for them, and re-layouts: 8.58 us -> 3.19 us
  starting transfers between devices: 3.6 us -> 0.04 us
    all_to_all x6 -> x3, blocking collectives: 210 us -> 137 us  [swap(): return lax.all_to_all(x, axis, split_axis=0, concat_axis=0, tiled=True)]
    reduce_scatter x1, waiting for transfers between devices: 0.01 us -> 56.9 us  [body(): summed = lax.psum_scatter(term, 'tensor', scatter_dimension=0, tiled=False)]
    all_gather x1, waiting for transfers between devices: 0.01 us -> 42.8 us  [body(): lax.all_gather(swap(sent, 'expert').reshape(expert_count, capacity * part...]
    all_to_all x1 -> x0, waiting for transfers between devices: 25.7 us -> none  [swap(): return lax.all_to_all(x, axis, split_axis=0, concat_axis=0, tiled=True)]
    reshape x7 -> x0, local copies, waits for them, and re-layouts: 6.71 us -> none  [the longest x4 3.91 us: to_experts(): pairs = sent.reshape(expert_count, 2, sent.shape[1] // 2)]
    pallas_call x2 -> x1, Pallas kernels: 16.4 us -> 10.1 us  [expert_layer(): pl.pallas_call(functools.partial(expert_kernel, steps), grid=(steps + cou...]
    all_to_all x1 -> x0, starting transfers between devices: 3.55 us -> none  [swap(): return lax.all_to_all(x, axis, split_axis=0, concat_axis=0, tiled=True)]
  transfers between devices with their start and end apart: 3 -> 2, of which waited for: 1 -> 2; matrix products, arithmetic and copies ran while one was open for 1% -> 0% of each run, Pallas kernels for 2% -> 0%
where the time goes in v4:
time: 271 us
  blocking collectives  137 us (51%)
  waiting for transfers between devices  99.8 us (37%)
  Pallas kernels  17.2 us (6%)
  between operations  13.5 us (5%)
  local copies, waits for them, and re-layouts  3.19 us (1%)
    all_to_all x3, blocking collectives, swap(): return lax.all_to_all(x, axis, split_axis=0, concat_axis=0, tiled=True)  137 us
    reduce_scatter x1, waiting for transfers between devices, body(): summed = lax.psum_scatter(term, 'tensor', scatter_dimension=0, tiled=False)  56.9 us
    all_gather x1, waiting for transfers between devices, body(): lax.all_gather(swap(sent, 'expert').reshape(expert_count, capacity * part...  42.8 us
    pallas_call x1, Pallas kernels, expert_layer(): pl.pallas_call(functools.partial(expert_kernel, steps), grid=(steps + cou...  10.1 us
  transfers between devices with their start and end apart: 2, of which 2 were waited for; matrix products, arithmetic and copies ran while one was open for 0% of the time, Pallas kernels for 0%

profile of v4, /device:TPU:1, one launch (start us, length us, event | category | flops | bytes accessed | tf_op | source)
XLA Modules:
  0.0 270.7 jit_solution(1232994612704671936)
XLA Ops:
  6.5 0.0 all-gather.2.cloned.1.call-start
  6.5 0.9 copy-done.1
  7.4 3.6 %project.1 = bf16[8,2,32,896]{3,2,1,0:T(8,128)(2,1)S(1)} custom-call(bf16[128,512]{1,0:T(8,128)(2,1)S(1)} %copy-done.1, bf16[512,3584]{1,0:T(8,128)(2,1)} %weight_ref.1), custom_call_target="tpu_custom_call" | custom-call | tf_op jit(solution)/shard_map/project/pallas_call | solution.py:40
  11.1 0.0 copy-start.5
  11.1 0.0 copy-start
  11.1 25.4 %all_to_all.15.parts_ref = bf16[16,32,896]{2,1,0:T(8,128)(2,1)S(1)} all-to-all(bf16[16,32,896]{2,1,0:T(8,128)(2,1)S(1)} %bitcast.6), channel_id=1, replica_groups=mesh['expert'=64,'tensor'=8,'dp'=2] {'tensor','dp'}, dimensions={0} | all-to-all | bytes 1835008 | tf_op jit(solution)/shard_map/all_to_all | solution.py:210
  36.5 0.0 copy-done.2
  36.5 0.0 copy-done.3
  36.5 1.2 dispatch.1
  37.7 62.8 %all_to_all.16 = bf16[64,2,1792]{2,1,0:T(2,128)(2,1)S(1)} all-to-all(bf16[64,2,1792]{2,1,0:T(2,128)(2,1)S(1)} %get-tuple-element.8), channel_id=1, replica_groups=mesh['expert'=64,'tensor'=8,'dp'=2] {'expert'}, dimensions={0} | all-to-all | bytes 917504 | tf_op jit(solution)/shard_map/all_to_all | solution.py:210
  100.5 1.1 all_gather_reshape.3
  101.6 0.0 all-gather.2.cloned.1.call-update
  101.6 0.0 reduce-scatter.2.cloned.1.call-start
  101.6 0.0 copy-done.5
  101.7 0.1 reshape.7.gain_ref
  101.7 42.8 %all-gather.2.cloned.1.call-done.x_ref = bf16[8,64,3584]{2,1,0:T(8,128)(2,1)} async-done(((bf16[1,64,3584]{2,1,0:T(8,128)(2,1)}), bf16[8,64,3584]{2,1,0:T(8,128)(2,1)}) %all-gather.2.cloned.1.call-update) | async-done | bytes 3670032 | tf_op jit(solution)/shard_map/all_gather | solution.py:243
  144.6 0.0 copy-done
  144.6 10.1 %expert_layer.1 = bf16[8,64,3584]{2,1,0:T(8,128)(2,1)} custom-call(bf16[8,64,3584]{2,1,0:T(8,128)(2,1)} %all-gather.2.cloned.1.call-done.x_ref, f32[8,1,448]{2,1,0:T(1,128)S(1)} %reshape.7.gain_ref, bf16[3584,256]{1,0:T(8,128)(2,1)S(1)} %bitcast.7, bf16[3584,256]{1,0:T(8,128)(2,1)} %bitcast.11, bf16[256,3584]{1,0:T(8,128)(2,1)} %bitcast.12), custom_call_target="tpu_custom_call" | custom-call | tf_op jit(solution)/shard_map/expert_layer/pallas_call | solution.py:163
  154.7 0.0 reduce-scatter.2.cloned.1.call-update
  154.7 56.9 %reduce-scatter.2.cloned.1.call-done = bf16[1,64,3584]{2,1,0:T(8,128)(2,1)} async-done(((bf16[8,64,3584]{2,1,0:T(8,128)(2,1)}), bf16[1,64,3584]{2,1,0:T(8,128)(2,1)}) %reduce-scatter.2.cloned.1.call-update) | async-done | bytes 458768 | tf_op jit(solution)/shard_map/reduce_scatter | solution.py:252
  211.6 1.1 reshape_reduce_scatter.3
  212.8 48.9 %all_to_all.17.returned_ref = bf16[64,2,1792]{2,1,0:T(2,128)(2,1)S(1)} all-to-all(bf16[64,2,1792]{2,1,0:T(2,128)(2,1)S(1)} %reshape_reduce_scatter.3), channel_id=1, replica_groups=mesh['expert'=64,'tensor'=8,'dp'=2] {'expert'}, dimensions={0} | all-to-all | bytes 917504 | tf_op jit(solution)/shard_map/all_to_all | solution.py:210
  261.6 0.0 copy-done.4
  261.6 2.2 combine.1
  (4 shorter events, 0.0 us)
Async XLA Ops:
  6.5 138.0 %all-gather.2.cloned.1.call-start = ((), (), s32[]{:S(2)}) async-start(), calls=%async_computation.4 | async-start | bytes 4128768 | tf_op jit(solution)/shard_map/all_gather | solution.py:243
  6.5 0.9 copy-start.1
  7.4 29.1 %copy-start.2 = (bf16[64,448]{1,0:T(8,128)(2,1)S(1)}, bf16[64,448]{1,0:T(8,128)(2,1)}, u32[]{:S(2)}) copy-start(bf16[64,448]{1,0:T(8,128)(2,1)} %residual_ref.1) | copy-start | bytes 172036
  7.4 29.1 %copy-start.3 = (s32[64,8]{0,1:T(8,128)S(1)}, s32[64,8]{0,1:T(8,128)}, u32[]{:S(2)}) copy-start(s32[64,8]{0,1:T(8,128)} %param.16) | copy-start | bytes 6148
  11.1 90.6 %copy-start.5 = (f32[3584]{0:T(1024)S(1)}, f32[3584]{0:T(1024)}, u32[]{:S(2)}) copy-start(f32[3584]{0:T(1024)} %param.12) | copy-start | bytes 43012
  11.1 133.5 %copy-start = (bf16[1,3584,256]{2,1,0:T(8,128)(2,1)S(1)}, bf16[1,3584,256]{2,1,0:T(8,128)(2,1)}, u32[]{:S(2)}) copy-start(bf16[1,3584,256]{2,1,0:T(8,128)(2,1)} %param.13) | copy-start | bytes 5505028
  101.6 110.0 %reduce-scatter.2.cloned.1.call-start = ((), (), s32[]{:S(2)}) async-start(), calls=%async_computation.5 | async-start | bytes 4128768 | tf_op jit(solution)/shard_map/reduce_scatter | solution.py:252
  154.7 106.9 %copy-start.4 = (s32[64,8]{0,1:T(8,128)S(1)}, s32[64,8]{0,1:T(8,128)}, u32[]{:S(2)}) copy-start(s32[64,8]{0,1:T(8,128)} %param.17) | copy-start | bytes 6148
Sparse Core Ops, SparseCore 0:
  101.7 42.8 all-gather.1
  154.9 56.7 reduce-scatter.1

commit v5 on v4

--- a/solution.py
+++ b/solution.py
@@ -6,6 +6,7 @@
 from jax.experimental import pallas as pl
 from jax.experimental.pallas import tpu as pltpu
 from jax.sharding import PartitionSpec as P
+
 
 norm_eps = 1e-06
 route_scale = 2.5
@@ -84,51 +85,84 @@
         sent_ref[:, :, g * part : (g + 1) * part] = jnp.concatenate(lines, axis=1).astype(bf16)
 
 
-def expert_kernel(steps, x_ref, gain_ref, gate_ref, up_ref, down_ref, out_ref, gate_acc, up_acc, square_acc, hidden):
+def pack_kernel(rank_ref, down_ref, *out_refs):
+    count = len(out_refs)
+    rows, wide = out_refs[0].shape
+    part = wide // 2
+    step = pl.program_id(0)
+    for j in range(2):
+        shift = lax.rem(2 * step + j + count - rank_ref[0], count)
+        for s in range(count):
+
+            @pl.when(shift == s)
+            def _():
+                for h in range(2):
+                    out_refs[s][:, h * part : (h + 1) * part] = down_ref[
+                        h * rows : (h + 1) * rows, j * part : (j + 1) * part
+                    ]
+
+
+def pack_down(down_weights, tensor_count, dp_count):
+    rows, width = down_weights.shape[0] // dp_count, down_weights.shape[1]
+    wide = 2 * (width // tensor_count)
+    rank = jnp.stack([lax.axis_index("tensor"), lax.axis_index("dp")]).astype(jnp.int32)
+    whole = pl.BlockSpec((rows // 2, wide), lambda s, rank_ref: (0, 0))
+    return pl.pallas_call(
+        pack_kernel,
+        grid_spec=pltpu.PrefetchScalarGridSpec(
+            num_scalar_prefetch=1,
+            grid=(tensor_count // 2,),
+            in_specs=[pl.BlockSpec((rows, wide), lambda s, rank_ref: (rank_ref[1], s))],
+            out_specs=[whole] * tensor_count,
+        ),
+        out_shape=[jax.ShapeDtypeStruct((rows // 2, wide), bf16)] * tensor_count,
+        compiler_params=pltpu.CompilerParams(vmem_limit_bytes=16 << 20),
+        name="pack_down",
+    )(rank, in_hbm(down_weights))
+
+
+def hidden_kernel(steps, x_ref, gain_ref, gate_ref, up_ref, out_ref, gate_acc, up_acc, square_acc):
     step = pl.program_id(0)
     slices, _, part = gain_ref.shape
     rows = x_ref.shape[1]
     segments = x_ref.shape[2] // part
     width = part * slices * steps
     lanes = square_acc.shape[1]
-
-    @pl.when(step < steps)
-    def _():
-        gate = up = None
-        square = [None] * segments
-        for k in range(slices):
-            scaled = []
-            for g in range(segments):
-                wide = x_ref[k, :, g * part : (g + 1) * part].astype(f32)
-                scaled.append((wide * gain_ref[k]).astype(bf16))
-                powers = wide * wide
-                for c in range(0, part, lanes):
-                    piece = powers[:, c : c + lanes]
-                    if piece.shape[1] < lanes:
-                        piece = jnp.concatenate(
-                            [piece, jnp.zeros((rows, lanes - piece.shape[1]), f32)], axis=1
-                        )
-                    square[g] = piece if square[g] is None else square[g] + piece
-            scaled = jnp.concatenate(scaled, axis=0)
-            depth = slice(k * part, (k + 1) * part)
-            whole_depth = pl.ds(pl.multiple_of((step * slices + k) * part, 64), part)
-            gate_term = mm(scaled, gate_ref[whole_depth, :])
-            up_term = mm(scaled, up_ref[depth, :])
-            gate = gate_term if gate is None else gate + gate_term
-            up = up_term if up is None else up + up_term
-        square = jnp.concatenate(square, axis=0)
-
-        @pl.when(step == 0)
-        def _():
-            gate_acc[...] = gate
-            up_acc[...] = up
-            square_acc[...] = square
-
-        @pl.when(step > 0)
-        def _():
-            gate_acc[...] += gate
-            up_acc[...] += up
-            square_acc[...] += square
+    gate = up = None
+    square = [None] * segments
+    for k in range(slices):
+        scaled = []
+        for g in range(segments):
+            wide = x_ref[k, :, g * part : (g + 1) * part].astype(f32)
+            scaled.append((wide * gain_ref[k]).astype(bf16))
+            powers = wide * wide
+            for c in range(0, part, lanes):
+                piece = powers[:, c : c + lanes]
+                if piece.shape[1] < lanes:
+                    piece = jnp.concatenate(
+                        [piece, jnp.zeros((rows, lanes - piece.shape[1]), f32)], axis=1
+                    )
+                square[g] = piece if square[g] is None else square[g] + piece
+        scaled = jnp.concatenate(scaled, axis=0)
+        depth = slice(k * part, (k + 1) * part)
+        whole_depth = pl.ds(pl.multiple_of((step * slices + k) * part, 64), part)
+        gate_term = mm(scaled, gate_ref[whole_depth, :])
+        up_term = mm(scaled, up_ref[depth, :])
+        gate = gate_term if gate is None else gate + gate_term
+        up = up_term if up is None else up + up_term
+    square = jnp.concatenate(square, axis=0)
+
+    @pl.when(step == 0)
+    def _():
+        gate_acc[...] = gate
+        up_acc[...] = up
+        square_acc[...] = square
+
+    @pl.when(step > 0)
+    def _():
+        gate_acc[...] += gate
+        up_acc[...] += up
+        square_acc[...] += square
 
     @pl.when(step == steps - 1)
     def _():
@@ -136,51 +170,101 @@
         inverse = lax.rsqrt(mean + norm_eps)
         gate = inverse * gate_acc[...]
         up = inverse * up_acc[...]
-        hidden[...] = (jax.nn.silu(gate) * up).astype(bf16)
-
-    @pl.when(step >= steps)
-    def _():
-        for j in range(0, out_ref.shape[0], 2):
-            term = mm(hidden[...], down_ref[:, j * part : (j + 2) * part]).astype(bf16)
-            for g in range(segments):
-                for i in range(2):
-                    out_ref[j + i, :, g * part : (g + 1) * part] = term[
-                        g * rows : (g + 1) * rows, i * part : (i + 1) * part
-                    ]
-
-
-def expert_layer(x, gain, gate_weights, up_weights, down_weights):
+        out_ref[...] = (jax.nn.silu(gate) * up).astype(bf16)
+
+
+def hidden_units(x, gain, gate_weights, up_weights):
     count, rows, wide = x.shape
     width, hidden_width = gate_weights.shape
     part = width // count
     total_rows = rows * (wide // part)
-    slices, outs = 2, 4
+    slices = 2
     steps = count // slices
-
-    def late(s):
-        return jnp.maximum(s - steps, 0)
-
-    return pl.pallas_call(
-        functools.partial(expert_kernel, steps),
-        grid=(steps + count // outs,),
+    return pl.pallas_call(
+        functools.partial(hidden_kernel, steps),
+        grid=(steps,),
         in_specs=[
-            pl.BlockSpec((slices, rows, wide), lambda s: (jnp.minimum(s, steps - 1), 0, 0)),
-            pl.BlockSpec((slices, 1, part), lambda s: (jnp.minimum(s, steps - 1), 0, 0)),
+            pl.BlockSpec((slices, rows, wide), lambda s: (s, 0, 0)),
+            pl.BlockSpec((slices, 1, part), lambda s: (s, 0, 0)),
             pl.BlockSpec(memory_space=pltpu.VMEM),
-            pl.BlockSpec((slices * part, hidden_width), lambda s: (jnp.minimum(s, steps - 1), 0)),
-            pl.BlockSpec((hidden_width, outs * part), lambda s: (0, late(s))),
+            pl.BlockSpec((slices * part, hidden_width), lambda s: (s, 0)),
         ],
-        out_specs=pl.BlockSpec((outs, rows, wide), lambda s: (late(s), 0, 0)),
-        out_shape=pltpu.HBM((count, rows, wide), bf16),
+        out_specs=pl.BlockSpec((total_rows, hidden_width), lambda s: (0, 0)),
+        out_shape=pltpu.HBM((total_rows, hidden_width), bf16),
         scratch_shapes=[
             pltpu.VMEM((total_rows, hidden_width), f32),
             pltpu.VMEM((total_rows, hidden_width), f32),
             pltpu.VMEM((total_rows, 128), f32),
-            pltpu.VMEM((total_rows, hidden_width), bf16),
         ],
         compiler_params=pltpu.CompilerParams(vmem_limit_bytes=28 << 20),
-        name="expert_layer",
-    )(x, gain.reshape(count, 1, part), gate_weights, up_weights, down_weights)
+        name="hidden_units",
+    )(x, gain.reshape(count, 1, part), gate_weights, up_weights)
+
+
+def output_kernel(steps, rank_ref, first_ref, second_ref, low_ref, high_ref, out_ref, acc):
+    step = pl.program_id(0)
+    rows = out_ref.shape[0]
+    part = acc.shape[1]
+    segments = out_ref.shape[2] // part
+    total = None
+    for k, hidden_ref in enumerate((first_ref, second_ref)):
+        down = jnp.concatenate(
+            [
+                ref[k, :, h * part : (h + 1) * part]
+                for ref in (low_ref, high_ref)
+                for h in range(2)
+            ],
+            axis=0,
+        )
+        term = mm(hidden_ref[0], down)
+        total = term if total is None else total + term
+
+    @pl.when(step == 0)
+    def _():
+        acc[...] = total
+
+    @pl.when(step > 0)
+    def _():
+        acc[...] += total
+
+    @pl.when(step == steps - 1)
+    def _():
+        for g in range(segments):
+            lines = [
+                acc[(i * segments + g) * rows : (i * segments + g + 1) * rows, :][:, None, :]
+                for i in range(2)
+            ]
+            out_ref[:, :, g * part : (g + 1) * part] = jnp.concatenate(lines, axis=1).astype(bf16)
+
+
+def expert_outputs(hidden, low, high, out_rows):
+    count, total_rows, depth = hidden.shape
+    _, quarter, wide = low.shape
+    part = wide // 2
+    steps = count // 2
+    rank = lax.axis_index("tensor").astype(jnp.int32).reshape(1)
+    half_wide = total_rows // out_rows // 2 * part
+
+    def block(k):
+        return pl.BlockSpec(
+            (1, total_rows, depth),
+            lambda s, rank_ref: (lax.rem(rank_ref[0] + count - (2 * s + k), count), 0, 0),
+        )
+
+    pieces = pl.BlockSpec((2, quarter, wide), lambda s, rank_ref: (s, 0, 0))
+    return pl.pallas_call(
+        functools.partial(output_kernel, steps),
+        grid_spec=pltpu.PrefetchScalarGridSpec(
+            num_scalar_prefetch=1,
+            grid=(steps,),
+            in_specs=[block(0), block(1), pieces, pieces],
+            out_specs=pl.BlockSpec((out_rows, 2, half_wide), lambda s, rank_ref: (0, 0, 0)),
+            scratch_shapes=[pltpu.VMEM((total_rows, part), f32)],
+        ),
+        out_shape=jax.ShapeDtypeStruct((out_rows, 2, half_wide), bf16),
+        compiler_params=pltpu.CompilerParams(vmem_limit_bytes=28 << 20),
+        name="expert_outputs",
+    )(rank, hidden, hidden, low, high)
 
 
 def combine_kernel(stream_ref, routes_ref, values_ref, returned_ref, out_ref):
@@ -240,17 +324,31 @@
         name="dispatch",
     )(parts, residual, routes.T)
 
+    packed = pack_down(down_weights[0], tensor_count, dp_count)
+    sent, *packed = lax.optimization_barrier((sent, *packed))
+    received = swap(sent, "expert")
+    rolled = [
+        lax.ppermute(piece, "tensor", [(i, (i + s) % tensor_count) for i in range(tensor_count)])
+        if s
+        else piece
+        for s, piece in enumerate(packed)
+    ]
     whole = lax.all_gather(
-        swap(sent, "expert").reshape(expert_count, capacity * part), "tensor", axis=0, tiled=False)
-    term = expert_layer(
+        received.reshape(expert_count, capacity * part), "tensor", axis=0, tiled=False
+    )
+    hidden = hidden_units(
         in_hbm(whole),
         norm_gain,
         pltpu.with_memory_space_constraint(gate_weights[0], pltpu.VMEM),
         in_hbm(up_weights[0]),
-        in_hbm(down_weights[0]),
     )
-    summed = lax.psum_scatter(term, "tensor", scatter_dimension=0, tiled=False)
-    returned = swap(summed.reshape(expert_count, 2, capacity // 2 * part), "expert")
+    hidden_all = lax.all_gather(hidden, "tensor", axis=0, tiled=False)
+    mine = jnp.stack(rolled)
+    theirs = lax.ppermute(mine, "dp", [(0, 1), (1, 0)])
+    first = lax.axis_index("dp") == 0
+    low = jnp.where(first, mine, theirs)
+    high = jnp.where(first, theirs, mine)
+    returned = swap(expert_outputs(in_hbm(hidden_all), low, high, expert_count), "expert")
     return pl.pallas_call(
         combine_kernel,
         out_shape=jax.ShapeDtypeStruct((own_tokens, part), bf16),

time: 271 us -> 286 us (1.055)
  starting transfers between devices: 0.04 us -> 37.7 us
  blocking collectives: 137 us -> 116 us
  waiting for transfers between devices: 99.8 us -> 89.3 us
  Pallas kernels: 17.2 us -> 23.3 us
    reduce_scatter x1 -> x0, waiting for transfers between devices: 56.9 us -> none  [body(): summed = lax.psum_scatter(term, 'tensor', scatter_dimension=0, tiled=False)]
    ppermute x0 -> x8, waiting for transfers between devices: none -> 35.9 us  [the longest x7 18.5 us: body(): lax.ppermute(piece, 'tensor', [(i, (i + s) % tensor_count) for i in range...]
    ppermute x0 -> x8, starting transfers between devices: none -> 28.8 us  [the longest x7 25.8 us: body(): lax.ppermute(piece, 'tensor', [(i, (i + s) % tensor_count) for i in range...]
    all_to_all x3 -> x2, blocking collectives: 137 us -> 116 us  [swap(): return lax.all_to_all(x, axis, split_axis=0, concat_axis=0, tiled=True)]
    all_to_all x0 -> x1, waiting for transfers between devices: none -> 10.7 us  [swap(): return lax.all_to_all(x, axis, split_axis=0, concat_axis=0, tiled=True)]
    all_to_all x0 -> x1, starting transfers between devices: none -> 8.8 us  [swap(): return lax.all_to_all(x, axis, split_axis=0, concat_axis=0, tiled=True)]
    pallas_call x1 -> x3, Pallas kernels: 10.1 us -> 15.3 us  [the longest x1 7.3 us: hidden_units(): pl.pallas_call(functools.partial(hidden_kernel, steps), grid=(steps,), in...]
    all_gather x1 -> x2, waiting for transfers between devices: 42.8 us -> 42.6 us  [the longest x1 42.6 us: body(): lax.all_gather(received.reshape(expert_count, capacity * part), 'tensor',...]
  transfers between devices with their start and end apart: 2 -> 11, of which waited for: 2 -> 6; matrix products, arithmetic and copies ran while one was open for 0% -> 1% of each run, Pallas kernels for 0% -> 1%
where the time goes in v5:
time: 286 us; the launch traced here: 285 us
  blocking collectives  116 us (41%)
  waiting for transfers between devices  89.3 us (31%)
  starting transfers between devices  37.7 us (13%)
  Pallas kernels  23.3 us (8%)
  between operations  13.7 us (5%)
  local copies, waits for them, and re-layouts  4.14 us (1%)
    all_to_all x2, blocking collectives, swap(): return lax.all_to_all(x, axis, split_axis=0, concat_axis=0, tiled=True)  116 us
    all_gather x1, waiting for transfers between devices, body(): lax.all_gather(received.reshape(expert_count, capacity * part), 'tensor',...  42.6 us
    ppermute x7, starting transfers between devices, body(): lax.ppermute(piece, 'tensor', [(i, (i + s) % tensor_count) for i in range...  25.8 us
    ppermute x7, waiting for transfers between devices, body(): lax.ppermute(piece, 'tensor', [(i, (i + s) % tensor_count) for i in range...  18.5 us
    ppermute x1, waiting for transfers between devices, body(): theirs = lax.ppermute(mine, 'dp', [(0, 1), (1, 0)])  17.4 us
    all_to_all x1, waiting for transfers between devices, swap(): return lax.all_to_all(x, axis, split_axis=0, concat_axis=0, tiled=True)  10.7 us
    all_to_all x1, starting transfers between devices, swap(): return lax.all_to_all(x, axis, split_axis=0, concat_axis=0, tiled=True)  8.8 us
    pallas_call x1, Pallas kernels, hidden_units(): pl.pallas_call(functools.partial(hidden_kernel, steps), grid=(steps,), in...  7.3 us
  transfers between devices with their start and end apart: 11, of which 6 were waited for; matrix products, arithmetic and copies ran while one was open for 1% of the time, Pallas kernels for 1%

profile of v5, /device:TPU:1, one launch (start us, length us, event | category | flops | bytes accessed | tf_op | source)
XLA Modules:
  0.0 285.0 jit_solution(5587082948460888350)
XLA Ops:
  7.4 4.6 %project.1 = bf16[8,2,32,896]{3,2,1,0:T(8,128)(2,1)} custom-call(bf16[128,512]{1,0:T(8,128)(2,1)S(1)} %copy-done.1, bf16[512,3584]{1,0:T(8,128)(2,1)} %weight_ref.1), custom_call_target="tpu_custom_call" | custom-call | tf_op jit(solution)/shard_map/project/pallas_call | solution.py:41
  12.0 8.8 %all-to-all-start = ((bf16[16,32,896]{2,1,0:T(8,128)(2,1)}), bf16[16,32,896]{2,1,0:T(8,128)(2,1)S(1)}, u32[]{:S(2)}, u32[]{:S(2)}) async-start(bf16[16,32,896]{2,1,0:T(8,128)(2,1)} %bitcast), calls=%async_computation | async-start | bytes 1835008 | tf_op jit(solution)/shard_map/all_to_all | solution.py:294
  20.9 3.2 %pack_down.1 = (bf16[64,896]{1,0:T(8,128)(2,1)S(1)}, bf16[64,896]{1,0:T(8,128)(2,1)S(1)}, bf16[64,896]{1,0:T(8,128)(2,1)S(1)}, bf16[64,896]{1,0:T(8,128)(2,1)S(1...) custom-call(s32[2]{0:T(128)S(1)} %pad_add_fusion.rank_ref, ...), custom_call_target="tpu_custom_call" | custom-call | tf_op jit(solution)/shard_map/pack_down/pallas_call | solution.py:110
  26.1 10.7 %all-to-all-done.parts_ref = bf16[16,32,896]{2,1,0:T(8,128)(2,1)S(1)} async-done(((bf16[16,32,896]{2,1,0:T(8,128)(2,1)}), bf16[16,32,896]{2,1,0:T(8,128)(2,1)S(1)}, u32[]{:S(2)}, u32[]{:S(2)}) %all-to-all-start) | async-done | bytes 917536 | tf_op jit(solution)/shard_map/all_to_all | solution.py:294
  36.9 1.2 dispatch.1
  38.0 63.8 %all_to_all.15 = bf16[64,2,1792]{2,1,0:T(2,128)(2,1)S(1)} all-to-all(bf16[64,2,1792]{2,1,0:T(2,128)(2,1)S(1)} %get-tuple-element.34), channel_id=1, replica_groups=mesh['expert'=64,'tensor'=8,'dp'=2] {'expert'}, dimensions={0} | all-to-all | bytes 917504 | tf_op jit(solution)/shard_map/all_to_all | solution.py:294
  103.1 42.6 %all-gather.4.cloned.1.call-done.x_ref = bf16[8,64,3584]{2,1,0:T(8,128)(2,1)} async-done(((bf16[1,64,3584]{2,1,0:T(8,128)(2,1)}), bf16[8,64,3584]{2,1,0:T(8,128)(2,1)}) %all-gather.4.cloned.1.call-update) | async-done | bytes 3670032 | tf_op jit(solution)/shard_map/all_gather | solution.py:336
  145.7 7.3 %hidden_units.1 = bf16[512,256]{1,0:T(8,128)(2,1)} custom-call(bf16[8,64,3584]{2,1,0:T(8,128)(2,1)} %all-gather.4.cloned.1.call-done.x_ref, f32[8,1,448]{2,1,0:T(1,128)S(1)} %reshape.11.gain_ref, bf16[3584,256]{1,0:T(8,128)(2,1)S(1)} %bitcast.25, bf16[3584,256]{1,0:T(8,128)(2,1)} %bitcast.32), custom_call_target="tpu_custom_call" | custom-call | tf_op jit(solution)/shard_map/hidden_units/pallas_call | solution.py:183
  153.0 1.9 collective-permute-start
  155.0 5.1 %collective-permute-start.1 = (bf16[64,896]{1,0:T(8,128)(2,1)S(1)}, bf16[64,896]{1,0:T(8,128)(2,1)S(1)}, u32[]{:S(2)}, u32[]{:S(2)}) collective-permute-start(bf16[64,896]{1,0:T(8,128)(2,1)S(1)} %copy-done.8), channel_id=1, source_target_pairs={{0,4},{2,6},{4,8},{6,10},{8,12},{10,14},{12,0},{14,2},{1,5},{3,7},... | collective-permute-start | bytes 344072 | tf_op jit(solution)/shard_map/ppermute | solution.py:331
  160.0 3.2 %collective-permute-start.2 = (bf16[64,896]{1,0:T(8,128)(2,1)S(1)}, bf16[64,896]{1,0:T(8,128)(2,1)S(1)}, u32[]{:S(2)}, u32[]{:S(2)}) collective-permute-start(bf16[64,896]{1,0:T(8,128)(2,1)S(1)} %copy-done.6), channel_id=1, source_target_pairs={{0,6},{2,8},{4,10},{6,12},{8,14},{10,0},{12,2},{14,4},{1,7},{3,9},... | collective-permute-start | bytes 344072 | tf_op jit(solution)/shard_map/ppermute | solution.py:331
  163.2 4.2 %collective-permute-start.3 = (bf16[64,896]{1,0:T(8,128)(2,1)S(1)}, bf16[64,896]{1,0:T(8,128)(2,1)S(1)}, u32[]{:S(2)}, u32[]{:S(2)}) collective-permute-start(bf16[64,896]{1,0:T(8,128)(2,1)S(1)} %get-tuple-element.39), channel_id=1, source_target_pairs={{0,8},{2,10},{4,12},{6,14},{8,0},{10,2},{12,4},{14,6},{1,9},{3,11}... | collective-permute-start | bytes 344072 | tf_op jit(solution)/shard_map/ppermute | solution.py:331
  167.4 4.1 %collective-permute-start.4 = (bf16[64,896]{1,0:T(8,128)(2,1)S(1)}, bf16[64,896]{1,0:T(8,128)(2,1)S(1)}, u32[]{:S(2)}, u32[]{:S(2)}) collective-permute-start(bf16[64,896]{1,0:T(8,128)(2,1)S(1)} %get-tuple-element.40), channel_id=1, source_target_pairs={{0,10},{2,12},{4,14},{6,0},{8,2},{10,4},{12,6},{14,8},{1,11},{3,13... | collective-permute-start | bytes 344072 | tf_op jit(solution)/shard_map/ppermute | solution.py:331
  171.5 5.2 %collective-permute-start.5 = (bf16[64,896]{1,0:T(8,128)(2,1)S(1)}, bf16[64,896]{1,0:T(8,128)(2,1)S(1)}, u32[]{:S(2)}, u32[]{:S(2)}) collective-permute-start(bf16[64,896]{1,0:T(8,128)(2,1)S(1)} %get-tuple-element.41), channel_id=1, source_target_pairs={{0,12},{2,14},{4,0},{6,2},{8,4},{10,6},{12,8},{14,10},{1,13},{3,15... | collective-permute-start | bytes 344072 | tf_op jit(solution)/shard_map/ppermute | solution.py:331
  176.8 2.2 collective-permute-start.6
  179.0 4.1 %collective-permute-done.4 = bf16[64,896]{1,0:T(8,128)(2,1)S(1)} collective-permute-done((bf16[64,896]{1,0:T(8,128)(2,1)S(1)}, bf16[64,896]{1,0:T(8,128)(2,1)S(1)}, u32[]{:S(2)}, u32[]{:S(2)}) %collective-permute-start.4) | collective-permute-done | bytes 114720 | tf_op jit(solution)/shard_map/ppermute | solution.py:331
  183.1 9.9 %collective-permute-done.5 = bf16[64,896]{1,0:T(8,128)(2,1)S(1)} collective-permute-done((bf16[64,896]{1,0:T(8,128)(2,1)S(1)}, bf16[64,896]{1,0:T(8,128)(2,1)S(1)}, u32[]{:S(2)}, u32[]{:S(2)}) %collective-permute-start.5) | collective-permute-done | bytes 114720 | tf_op jit(solution)/shard_map/ppermute | solution.py:331
  193.0 4.6 %collective-permute-done.6 = bf16[64,896]{1,0:T(8,128)(2,1)S(1)} collective-permute-done((bf16[64,896]{1,0:T(8,128)(2,1)S(1)}, bf16[64,896]{1,0:T(8,128)(2,1)S(1)}, u32[]{:S(2)}, u32[]{:S(2)}) %collective-permute-start.6) | collective-permute-done | bytes 114720 | tf_op jit(solution)/shard_map/ppermute | solution.py:331
  197.6 3.0 %collective-permute-start.7 = (bf16[8,64,896]{2,1,0:T(8,128)(2,1)S(1)}, bf16[8,64,896]{2,1,0:T(8,128)(2,1)}, u32[]{:S(2)}, u32[]{:S(2)}) collective-permute-start(bf16[8,64,896]{2,1,0:T(8,128)(2,1)S(1)} %bitcast_dynamic-update-slice_fusion), channel_id=1, source_target_pairs={{0,1},{1,0},{2,3},{3,2},{4,5},{5,4},{6,7},{7,6},{8,9},{9,8},{10,11... | collective-permute-start | bytes 2752520 | tf_op jit(solution)/shard_map/ppermute | solution.py:347
  200.6 17.4 %collective-permute-done.7 = bf16[8,64,896]{2,1,0:T(8,128)(2,1)} collective-permute-done((bf16[8,64,896]{2,1,0:T(8,128)(2,1)S(1)}, bf16[8,64,896]{2,1,0:T(8,128)(2,1)}, u32[]{:S(2)}, u32[]{:S(2)}) %collective-permute-start.7) | collective-permute-done | bytes 917536 | tf_op jit(solution)/shard_map/ppermute | solution.py:347
  218.0 1.4 broadcast_select_fusion
  219.4 4.8 %expert_outputs.1 = bf16[64,2,1792]{2,1,0:T(2,128)(2,1)S(1)} custom-call(s32[1]{0:T(128)} %bitcast.3.rank_ref, bf16[8,512,256]{2,1,0:T(8,128)(2,1)} %bitcast.29, bf16[8,512,256]{2,1,0:T(8,128)(2,1)} %bitcast.30, bf16[8,64,896]{2,1,0:T(8,128)(2,1)S(1)} %get-tuple-element.44.low_ref, bf16[8,64,896]{2,1,0:T(8,128)(2,1)S(1)} %get-tuple-element.43.high_ref), custom_call_target="tpu_custom_call" | custom-call | tf_op jit(solution)/shard_map/expert_outputs/pallas_call | solution.py:255
  224.2 51.8 %all_to_all.16.returned_ref = bf16[64,2,1792]{2,1,0:T(2,128)(2,1)S(1)} all-to-all(bf16[64,2,1792]{2,1,0:T(2,128)(2,1)S(1)} %expert_outputs.1), channel_id=1, replica_groups=mesh['expert'=64,'tensor'=8,'dp'=2] {'expert'}, dimensions={0} | all-to-all | bytes 917504 | tf_op jit(solution)/shard_map/all_to_all | solution.py:294
  276.0 2.2 combine.1
  (44 shorter events, 4.4 us)
Async XLA Ops:
  6.5 0.9 copy-start.1
  12.0 24.9 %copy-start.2 = (bf16[64,448]{1,0:T(8,128)(2,1)S(1)}, bf16[64,448]{1,0:T(8,128)(2,1)}, u32[]{:S(2)}) copy-start(bf16[64,448]{1,0:T(8,128)(2,1)} %residual_ref.1) | copy-start | bytes 172036
  12.0 24.9 %copy-start.3 = (s32[64,8]{0,1:T(8,128)S(1)}, s32[64,8]{0,1:T(8,128)}, u32[]{:S(2)}) copy-start(s32[64,8]{0,1:T(8,128)} %param.16) | copy-start | bytes 6148
  12.0 24.8 %all-to-all-start = ((bf16[16,32,896]{2,1,0:T(8,128)(2,1)}), bf16[16,32,896]{2,1,0:T(8,128)(2,1)S(1)}, u32[]{:S(2)}, u32[]{:S(2)}) async-start(bf16[16,32,896]{2,1,0:T(8,128)(2,1)} %bitcast), calls=%async_computation | async-start | bytes 1835008 | tf_op jit(solution)/shard_map/all_to_all | solution.py:294
  20.8 124.9 %all-gather.4.cloned.1.call-start = ((), (), s32[]{:S(2)}) async-start(), calls=%async_computation.3 | async-start | bytes 4128768 | tf_op jit(solution)/shard_map/all_gather | solution.py:336
  24.2 0.7 copy-start.5
  24.8 0.7 copy-start.7
  25.5 0.6 copy-start.9
  26.1 76.9 %copy-start.11 = (f32[3584]{0:T(1024)S(1)}, f32[3584]{0:T(1024)}, u32[]{:S(2)}) copy-start(f32[3584]{0:T(1024)} %param.12) | copy-start | bytes 43012
  26.1 119.5 %copy-start = (bf16[1,3584,256]{2,1,0:T(8,128)(2,1)S(1)}, bf16[1,3584,256]{2,1,0:T(8,128)(2,1)}, u32[]{:S(2)}) copy-start(bf16[1,3584,256]{2,1,0:T(8,128)(2,1)} %param.13) | copy-start | bytes 5505028
  102.9 116.5 %all-gather.6.cloned.1.call-start = ((), (), s32[]{:S(2)}) async-start(), calls=%async_computation.4 | async-start | bytes 2359296 | tf_op jit(solution)/shard_map/all_gather | solution.py:345
  145.7 7.3 %copy-start.10 = (bf16[64,896]{1,0:T(8,128)(2,1)S(1)}, bf16[64,896]{1,0:T(8,128)(2,1)}, u32[]{:S(2)}) copy-start(bf16[64,896]{1,0:T(8,128)(2,1)} %copy-done.9) | copy-start | bytes 344068
  145.7 9.3 %copy-start.8 = (bf16[64,896]{1,0:T(8,128)(2,1)S(1)}, bf16[64,896]{1,0:T(8,128)(2,1)}, u32[]{:S(2)}) copy-start(bf16[64,896]{1,0:T(8,128)(2,1)} %copy-done.7) | copy-start | bytes 344068
  145.7 14.3 %copy-start.6 = (bf16[64,896]{1,0:T(8,128)(2,1)S(1)}, bf16[64,896]{1,0:T(8,128)(2,1)}, u32[]{:S(2)}) copy-start(bf16[64,896]{1,0:T(8,128)(2,1)} %copy-done.5) | copy-start | bytes 344068
  153.0 18.5 %collective-permute-start = (bf16[64,896]{1,0:T(8,128)(2,1)S(1)}, bf16[64,896]{1,0:T(8,128)(2,1)S(1)}, u32[]{:S(2)}, u32[]{:S(2)}) collective-permute-start(bf16[64,896]{1,0:T(8,128)(2,1)S(1)} %copy-done.10), channel_id=1, source_target_pairs={{0,2},{2,4},{4,6},{6,8},{8,10},{10,12},{12,14},{14,0},{1,3},{3,5},... | collective-permute-start | bytes 344072 | tf_op jit(solution)/shard_map/ppermute | solution.py:331
  155.0 21.8 %collective-permute-start.1 = (bf16[64,896]{1,0:T(8,128)(2,1)S(1)}, bf16[64,896]{1,0:T(8,128)(2,1)S(1)}, u32[]{:S(2)}, u32[]{:S(2)}) collective-permute-start(bf16[64,896]{1,0:T(8,128)(2,1)S(1)} %copy-done.8), channel_id=1, source_target_pairs={{0,4},{2,6},{4,8},{6,10},{8,12},{10,14},{12,0},{14,2},{1,5},{3,7},... | collective-permute-start | bytes 344072 | tf_op jit(solution)/shard_map/ppermute | solution.py:331
  160.0 18.9 %collective-permute-start.2 = (bf16[64,896]{1,0:T(8,128)(2,1)S(1)}, bf16[64,896]{1,0:T(8,128)(2,1)S(1)}, u32[]{:S(2)}, u32[]{:S(2)}) collective-permute-start(bf16[64,896]{1,0:T(8,128)(2,1)S(1)} %copy-done.6), channel_id=1, source_target_pairs={{0,6},{2,8},{4,10},{6,12},{8,14},{10,0},{12,2},{14,4},{1,7},{3,9},... | collective-permute-start | bytes 344072 | tf_op jit(solution)/shard_map/ppermute | solution.py:331
  163.2 15.8 %collective-permute-start.3 = (bf16[64,896]{1,0:T(8,128)(2,1)S(1)}, bf16[64,896]{1,0:T(8,128)(2,1)S(1)}, u32[]{:S(2)}, u32[]{:S(2)}) collective-permute-start(bf16[64,896]{1,0:T(8,128)(2,1)S(1)} %get-tuple-element.39), channel_id=1, source_target_pairs={{0,8},{2,10},{4,12},{6,14},{8,0},{10,2},{12,4},{14,6},{1,9},{3,11}... | collective-permute-start | bytes 344072 | tf_op jit(solution)/shard_map/ppermute | solution.py:331
  167.4 15.7 %collective-permute-start.4 = (bf16[64,896]{1,0:T(8,128)(2,1)S(1)}, bf16[64,896]{1,0:T(8,128)(2,1)S(1)}, u32[]{:S(2)}, u32[]{:S(2)}) collective-permute-start(bf16[64,896]{1,0:T(8,128)(2,1)S(1)} %get-tuple-element.40), channel_id=1, source_target_pairs={{0,10},{2,12},{4,14},{6,0},{8,2},{10,4},{12,6},{14,8},{1,11},{3,13... | collective-permute-start | bytes 344072 | tf_op jit(solution)/shard_map/ppermute | solution.py:331
  171.5 21.4 %collective-permute-start.5 = (bf16[64,896]{1,0:T(8,128)(2,1)S(1)}, bf16[64,896]{1,0:T(8,128)(2,1)S(1)}, u32[]{:S(2)}, u32[]{:S(2)}) collective-permute-start(bf16[64,896]{1,0:T(8,128)(2,1)S(1)} %get-tuple-element.41), channel_id=1, source_target_pairs={{0,12},{2,14},{4,0},{6,2},{8,4},{10,6},{12,8},{14,10},{1,13},{3,15... | collective-permute-start | bytes 344072 | tf_op jit(solution)/shard_map/ppermute | solution.py:331
  176.8 20.8 %collective-permute-start.6 = (bf16[64,896]{1,0:T(8,128)(2,1)S(1)}, bf16[64,896]{1,0:T(8,128)(2,1)S(1)}, u32[]{:S(2)}, u32[]{:S(2)}) collective-permute-start(bf16[64,896]{1,0:T(8,128)(2,1)S(1)} %get-tuple-element.42), channel_id=1, source_target_pairs={{0,14},{2,0},{4,2},{6,4},{8,6},{10,8},{12,10},{14,12},{1,15},{3,1}... | collective-permute-start | bytes 344072 | tf_op jit(solution)/shard_map/ppermute | solution.py:331
  197.6 20.4 %collective-permute-start.7 = (bf16[8,64,896]{2,1,0:T(8,128)(2,1)S(1)}, bf16[8,64,896]{2,1,0:T(8,128)(2,1)}, u32[]{:S(2)}, u32[]{:S(2)}) collective-permute-start(bf16[8,64,896]{2,1,0:T(8,128)(2,1)S(1)} %bitcast_dynamic-update-slice_fusion), channel_id=1, source_target_pairs={{0,1},{1,0},{2,3},{3,2},{4,5},{5,4},{6,7},{7,6},{8,9},{9,8},{10,11... | collective-permute-start | bytes 2752520 | tf_op jit(solution)/shard_map/ppermute | solution.py:347
  219.4 56.5 %copy-start.4 = (s32[64,8]{0,1:T(8,128)S(1)}, s32[64,8]{0,1:T(8,128)}, u32[]{:S(2)}) copy-start(s32[64,8]{0,1:T(8,128)} %param.17) | copy-start | bytes 6148
Sparse Core Ops, SparseCore 0:
  103.1 42.5 all-gather.3
  153.1 59.0 all-gather.5

commit v6 on v5

--- a/solution.py
+++ b/solution.py
@@ -333,9 +333,8 @@
         else piece
         for s, piece in enumerate(packed)
     ]
-    whole = lax.all_gather(
-        received.reshape(expert_count, capacity * part), "tensor", axis=0, tiled=False
-    )
+    received = received.reshape(expert_count, capacity * part)
+    whole = lax.all_gather(received, "tensor", axis=0, tiled=False)
     hidden = hidden_units(
         in_hbm(whole),
         norm_gain,

time: 286 us -> 286 us (level)
  no operation moved by 1% of the time
where the time goes in v6:
time: 286 us; the launch traced here: 285 us
  blocking collectives  116 us (41%)
  waiting for transfers between devices  89.3 us (31%)
  starting transfers between devices  37.7 us (13%)
  Pallas kernels  23.3 us (8%)
  between operations  13.7 us (5%)
  local copies, waits for them, and re-layouts  4.14 us (1%)
    all_to_all x2, blocking collectives, swap(): return lax.all_to_all(x, axis, split_axis=0, concat_axis=0, tiled=True)  116 us
    all_gather x1, waiting for transfers between devices, body(): whole = lax.all_gather(received, 'tensor', axis=0, tiled=False)  42.6 us
    ppermute x7, starting transfers between devices, body(): lax.ppermute(piece, 'tensor', [(i, (i + s) % tensor_count) for i in range...  25.8 us
    ppermute x7, waiting for transfers between devices, body(): lax.ppermute(piece, 'tensor', [(i, (i + s) % tensor_count) for i in range...  18.5 us
    ppermute x1, waiting for transfers between devices, body(): theirs = lax.ppermute(mine, 'dp', [(0, 1), (1, 0)])  17.4 us
    all_to_all x1, waiting for transfers between devices, swap(): return lax.all_to_all(x, axis, split_axis=0, concat_axis=0, tiled=True)  10.7 us
    all_to_all x1, starting transfers between devices, swap(): return lax.all_to_all(x, axis, split_axis=0, concat_axis=0, tiled=True)  8.8 us
    pallas_call x1, Pallas kernels, hidden_units(): pl.pallas_call(functools.partial(hidden_kernel, steps), grid=(steps,), in...  7.3 us
  transfers between devices with their start and end apart: 11, of which 6 were waited for; matrix products, arithmetic and copies ran while one was open for 1% of the time, Pallas kernels for 1%

profile of v6, /device:TPU:1, one launch (start us, length us, event | category | flops | bytes accessed | tf_op | source)
XLA Modules:
  0.0 285.0 jit_solution(5587082948460888350)
XLA Ops:
  7.4 4.6 %project.1 = bf16[8,2,32,896]{3,2,1,0:T(8,128)(2,1)} custom-call(bf16[128,512]{1,0:T(8,128)(2,1)S(1)} %copy-done.1, bf16[512,3584]{1,0:T(8,128)(2,1)} %weight_ref.1), custom_call_target="tpu_custom_call" | custom-call | tf_op jit(solution)/shard_map/project/pallas_call | solution.py:41
  12.0 8.8 %all-to-all-start = ((bf16[16,32,896]{2,1,0:T(8,128)(2,1)}), bf16[16,32,896]{2,1,0:T(8,128)(2,1)S(1)}, u32[]{:S(2)}, u32[]{:S(2)}) async-start(bf16[16,32,896]{2,1,0:T(8,128)(2,1)} %bitcast), calls=%async_computation | async-start | bytes 1835008 | tf_op jit(solution)/shard_map/all_to_all | solution.py:294
  20.9 3.2 %pack_down.1 = (bf16[64,896]{1,0:T(8,128)(2,1)S(1)}, bf16[64,896]{1,0:T(8,128)(2,1)S(1)}, bf16[64,896]{1,0:T(8,128)(2,1)S(1)}, bf16[64,896]{1,0:T(8,128)(2,1)S(1...) custom-call(s32[2]{0:T(128)S(1)} %pad_add_fusion.rank_ref, ...), custom_call_target="tpu_custom_call" | custom-call | tf_op jit(solution)/shard_map/pack_down/pallas_call | solution.py:110
  26.1 10.7 %all-to-all-done.parts_ref = bf16[16,32,896]{2,1,0:T(8,128)(2,1)S(1)} async-done(((bf16[16,32,896]{2,1,0:T(8,128)(2,1)}), bf16[16,32,896]{2,1,0:T(8,128)(2,1)S(1)}, u32[]{:S(2)}, u32[]{:S(2)}) %all-to-all-start) | async-done | bytes 917536 | tf_op jit(solution)/shard_map/all_to_all | solution.py:294
  36.9 1.2 dispatch.1
  38.0 63.8 %all_to_all.15 = bf16[64,2,1792]{2,1,0:T(2,128)(2,1)S(1)} all-to-all(bf16[64,2,1792]{2,1,0:T(2,128)(2,1)S(1)} %get-tuple-element.34), channel_id=1, replica_groups=mesh['expert'=64,'tensor'=8,'dp'=2] {'expert'}, dimensions={0} | all-to-all | bytes 917504 | tf_op jit(solution)/shard_map/all_to_all | solution.py:294
  103.1 42.6 %all-gather.4.cloned.1.call-done.x_ref = bf16[8,64,3584]{2,1,0:T(8,128)(2,1)} async-done(((bf16[1,64,3584]{2,1,0:T(8,128)(2,1)}), bf16[8,64,3584]{2,1,0:T(8,128)(2,1)}) %all-gather.4.cloned.1.call-update) | async-done | bytes 3670032 | tf_op jit(solution)/shard_map/all_gather | solution.py:337
  145.7 7.3 %hidden_units.1 = bf16[512,256]{1,0:T(8,128)(2,1)} custom-call(bf16[8,64,3584]{2,1,0:T(8,128)(2,1)} %all-gather.4.cloned.1.call-done.x_ref, f32[8,1,448]{2,1,0:T(1,128)S(1)} %reshape.11.gain_ref, bf16[3584,256]{1,0:T(8,128)(2,1)S(1)} %bitcast.25, bf16[3584,256]{1,0:T(8,128)(2,1)} %bitcast.32), custom_call_target="tpu_custom_call" | custom-call | tf_op jit(solution)/shard_map/hidden_units/pallas_call | solution.py:183
  153.0 1.9 collective-permute-start
  155.0 5.1 %collective-permute-start.1 = (bf16[64,896]{1,0:T(8,128)(2,1)S(1)}, bf16[64,896]{1,0:T(8,128)(2,1)S(1)}, u32[]{:S(2)}, u32[]{:S(2)}) collective-permute-start(bf16[64,896]{1,0:T(8,128)(2,1)S(1)} %copy-done.8), channel_id=1, source_target_pairs={{0,4},{2,6},{4,8},{6,10},{8,12},{10,14},{12,0},{14,2},{1,5},{3,7},... | collective-permute-start | bytes 344072 | tf_op jit(solution)/shard_map/ppermute | solution.py:331
  160.0 3.2 %collective-permute-start.2 = (bf16[64,896]{1,0:T(8,128)(2,1)S(1)}, bf16[64,896]{1,0:T(8,128)(2,1)S(1)}, u32[]{:S(2)}, u32[]{:S(2)}) collective-permute-start(bf16[64,896]{1,0:T(8,128)(2,1)S(1)} %copy-done.6), channel_id=1, source_target_pairs={{0,6},{2,8},{4,10},{6,12},{8,14},{10,0},{12,2},{14,4},{1,7},{3,9},... | collective-permute-start | bytes 344072 | tf_op jit(solution)/shard_map/ppermute | solution.py:331
  163.2 4.2 %collective-permute-start.3 = (bf16[64,896]{1,0:T(8,128)(2,1)S(1)}, bf16[64,896]{1,0:T(8,128)(2,1)S(1)}, u32[]{:S(2)}, u32[]{:S(2)}) collective-permute-start(bf16[64,896]{1,0:T(8,128)(2,1)S(1)} %get-tuple-element.39), channel_id=1, source_target_pairs={{0,8},{2,10},{4,12},{6,14},{8,0},{10,2},{12,4},{14,6},{1,9},{3,11}... | collective-permute-start | bytes 344072 | tf_op jit(solution)/shard_map/ppermute | solution.py:331
  167.4 4.1 %collective-permute-start.4 = (bf16[64,896]{1,0:T(8,128)(2,1)S(1)}, bf16[64,896]{1,0:T(8,128)(2,1)S(1)}, u32[]{:S(2)}, u32[]{:S(2)}) collective-permute-start(bf16[64,896]{1,0:T(8,128)(2,1)S(1)} %get-tuple-element.40), channel_id=1, source_target_pairs={{0,10},{2,12},{4,14},{6,0},{8,2},{10,4},{12,6},{14,8},{1,11},{3,13... | collective-permute-start | bytes 344072 | tf_op jit(solution)/shard_map/ppermute | solution.py:331
  171.5 5.2 %collective-permute-start.5 = (bf16[64,896]{1,0:T(8,128)(2,1)S(1)}, bf16[64,896]{1,0:T(8,128)(2,1)S(1)}, u32[]{:S(2)}, u32[]{:S(2)}) collective-permute-start(bf16[64,896]{1,0:T(8,128)(2,1)S(1)} %get-tuple-element.41), channel_id=1, source_target_pairs={{0,12},{2,14},{4,0},{6,2},{8,4},{10,6},{12,8},{14,10},{1,13},{3,15... | collective-permute-start | bytes 344072 | tf_op jit(solution)/shard_map/ppermute | solution.py:331
  176.8 2.2 collective-permute-start.6
  179.0 4.1 %collective-permute-done.4 = bf16[64,896]{1,0:T(8,128)(2,1)S(1)} collective-permute-done((bf16[64,896]{1,0:T(8,128)(2,1)S(1)}, bf16[64,896]{1,0:T(8,128)(2,1)S(1)}, u32[]{:S(2)}, u32[]{:S(2)}) %collective-permute-start.4) | collective-permute-done | bytes 114720 | tf_op jit(solution)/shard_map/ppermute | solution.py:331
  183.1 9.9 %collective-permute-done.5 = bf16[64,896]{1,0:T(8,128)(2,1)S(1)} collective-permute-done((bf16[64,896]{1,0:T(8,128)(2,1)S(1)}, bf16[64,896]{1,0:T(8,128)(2,1)S(1)}, u32[]{:S(2)}, u32[]{:S(2)}) %collective-permute-start.5) | collective-permute-done | bytes 114720 | tf_op jit(solution)/shard_map/ppermute | solution.py:331
  193.0 4.6 %collective-permute-done.6 = bf16[64,896]{1,0:T(8,128)(2,1)S(1)} collective-permute-done((bf16[64,896]{1,0:T(8,128)(2,1)S(1)}, bf16[64,896]{1,0:T(8,128)(2,1)S(1)}, u32[]{:S(2)}, u32[]{:S(2)}) %collective-permute-start.6) | collective-permute-done | bytes 114720 | tf_op jit(solution)/shard_map/ppermute | solution.py:331
  197.6 3.0 %collective-permute-start.7 = (bf16[8,64,896]{2,1,0:T(8,128)(2,1)S(1)}, bf16[8,64,896]{2,1,0:T(8,128)(2,1)}, u32[]{:S(2)}, u32[]{:S(2)}) collective-permute-start(bf16[8,64,896]{2,1,0:T(8,128)(2,1)S(1)} %bitcast_dynamic-update-slice_fusion), channel_id=1, source_target_pairs={{0,1},{1,0},{2,3},{3,2},{4,5},{5,4},{6,7},{7,6},{8,9},{9,8},{10,11... | collective-permute-start | bytes 2752520 | tf_op jit(solution)/shard_map/ppermute | solution.py:346
  200.6 17.4 %collective-permute-done.7 = bf16[8,64,896]{2,1,0:T(8,128)(2,1)} collective-permute-done((bf16[8,64,896]{2,1,0:T(8,128)(2,1)S(1)}, bf16[8,64,896]{2,1,0:T(8,128)(2,1)}, u32[]{:S(2)}, u32[]{:S(2)}) %collective-permute-start.7) | collective-permute-done | bytes 917536 | tf_op jit(solution)/shard_map/ppermute | solution.py:346
  218.0 1.4 broadcast_select_fusion
  219.4 4.8 %expert_outputs.1 = bf16[64,2,1792]{2,1,0:T(2,128)(2,1)S(1)} custom-call(s32[1]{0:T(128)} %bitcast.3.rank_ref, bf16[8,512,256]{2,1,0:T(8,128)(2,1)} %bitcast.29, bf16[8,512,256]{2,1,0:T(8,128)(2,1)} %bitcast.30, bf16[8,64,896]{2,1,0:T(8,128)(2,1)S(1)} %get-tuple-element.44.low_ref, bf16[8,64,896]{2,1,0:T(8,128)(2,1)S(1)} %get-tuple-element.43.high_ref), custom_call_target="tpu_custom_call" | custom-call | tf_op jit(solution)/shard_map/expert_outputs/pallas_call | solution.py:255
  224.2 51.8 %all_to_all.16.returned_ref = bf16[64,2,1792]{2,1,0:T(2,128)(2,1)S(1)} all-to-all(bf16[64,2,1792]{2,1,0:T(2,128)(2,1)S(1)} %expert_outputs.1), channel_id=1, replica_groups=mesh['expert'=64,'tensor'=8,'dp'=2] {'expert'}, dimensions={0} | all-to-all | bytes 917504 | tf_op jit(solution)/shard_map/all_to_all | solution.py:294
  276.0 2.2 combine.1
  (44 shorter events, 4.4 us)
Async XLA Ops:
  6.5 0.9 copy-start.1
  12.0 24.9 %copy-start.2 = (bf16[64,448]{1,0:T(8,128)(2,1)S(1)}, bf16[64,448]{1,0:T(8,128)(2,1)}, u32[]{:S(2)}) copy-start(bf16[64,448]{1,0:T(8,128)(2,1)} %residual_ref.1) | copy-start | bytes 172036
  12.0 24.9 %copy-start.3 = (s32[64,8]{0,1:T(8,128)S(1)}, s32[64,8]{0,1:T(8,128)}, u32[]{:S(2)}) copy-start(s32[64,8]{0,1:T(8,128)} %param.16) | copy-start | bytes 6148
  12.0 24.8 %all-to-all-start = ((bf16[16,32,896]{2,1,0:T(8,128)(2,1)}), bf16[16,32,896]{2,1,0:T(8,128)(2,1)S(1)}, u32[]{:S(2)}, u32[]{:S(2)}) async-start(bf16[16,32,896]{2,1,0:T(8,128)(2,1)} %bitcast), calls=%async_computation | async-start | bytes 1835008 | tf_op jit(solution)/shard_map/all_to_all | solution.py:294
  20.8 124.9 %all-gather.4.cloned.1.call-start = ((), (), s32[]{:S(2)}) async-start(), calls=%async_computation.3 | async-start | bytes 4128768 | tf_op jit(solution)/shard_map/all_gather | solution.py:337
  24.2 0.7 copy-start.5
  24.8 0.7 copy-start.7
  25.5 0.6 copy-start.9
  26.1 76.9 %copy-start.11 = (f32[3584]{0:T(1024)S(1)}, f32[3584]{0:T(1024)}, u32[]{:S(2)}) copy-start(f32[3584]{0:T(1024)} %param.12) | copy-start | bytes 43012
  26.1 119.5 %copy-start = (bf16[1,3584,256]{2,1,0:T(8,128)(2,1)S(1)}, bf16[1,3584,256]{2,1,0:T(8,128)(2,1)}, u32[]{:S(2)}) copy-start(bf16[1,3584,256]{2,1,0:T(8,128)(2,1)} %param.13) | copy-start | bytes 5505028
  102.9 116.5 %all-gather.6.cloned.1.call-start = ((), (), s32[]{:S(2)}) async-start(), calls=%async_computation.4 | async-start | bytes 2359296 | tf_op jit(solution)/shard_map/all_gather | solution.py:344
  145.7 7.3 %copy-start.10 = (bf16[64,896]{1,0:T(8,128)(2,1)S(1)}, bf16[64,896]{1,0:T(8,128)(2,1)}, u32[]{:S(2)}) copy-start(bf16[64,896]{1,0:T(8,128)(2,1)} %copy-done.9) | copy-start | bytes 344068
  145.7 9.3 %copy-start.8 = (bf16[64,896]{1,0:T(8,128)(2,1)S(1)}, bf16[64,896]{1,0:T(8,128)(2,1)}, u32[]{:S(2)}) copy-start(bf16[64,896]{1,0:T(8,128)(2,1)} %copy-done.7) | copy-start | bytes 344068
  145.7 14.3 %copy-start.6 = (bf16[64,896]{1,0:T(8,128)(2,1)S(1)}, bf16[64,896]{1,0:T(8,128)(2,1)}, u32[]{:S(2)}) copy-start(bf16[64,896]{1,0:T(8,128)(2,1)} %copy-done.5) | copy-start | bytes 344068
  153.0 18.5 %collective-permute-start = (bf16[64,896]{1,0:T(8,128)(2,1)S(1)}, bf16[64,896]{1,0:T(8,128)(2,1)S(1)}, u32[]{:S(2)}, u32[]{:S(2)}) collective-permute-start(bf16[64,896]{1,0:T(8,128)(2,1)S(1)} %copy-done.10), channel_id=1, source_target_pairs={{0,2},{2,4},{4,6},{6,8},{8,10},{10,12},{12,14},{14,0},{1,3},{3,5},... | collective-permute-start | bytes 344072 | tf_op jit(solution)/shard_map/ppermute | solution.py:331
  155.0 21.8 %collective-permute-start.1 = (bf16[64,896]{1,0:T(8,128)(2,1)S(1)}, bf16[64,896]{1,0:T(8,128)(2,1)S(1)}, u32[]{:S(2)}, u32[]{:S(2)}) collective-permute-start(bf16[64,896]{1,0:T(8,128)(2,1)S(1)} %copy-done.8), channel_id=1, source_target_pairs={{0,4},{2,6},{4,8},{6,10},{8,12},{10,14},{12,0},{14,2},{1,5},{3,7},... | collective-permute-start | bytes 344072 | tf_op jit(solution)/shard_map/ppermute | solution.py:331
  160.0 18.9 %collective-permute-start.2 = (bf16[64,896]{1,0:T(8,128)(2,1)S(1)}, bf16[64,896]{1,0:T(8,128)(2,1)S(1)}, u32[]{:S(2)}, u32[]{:S(2)}) collective-permute-start(bf16[64,896]{1,0:T(8,128)(2,1)S(1)} %copy-done.6), channel_id=1, source_target_pairs={{0,6},{2,8},{4,10},{6,12},{8,14},{10,0},{12,2},{14,4},{1,7},{3,9},... | collective-permute-start | bytes 344072 | tf_op jit(solution)/shard_map/ppermute | solution.py:331
  163.2 15.8 %collective-permute-start.3 = (bf16[64,896]{1,0:T(8,128)(2,1)S(1)}, bf16[64,896]{1,0:T(8,128)(2,1)S(1)}, u32[]{:S(2)}, u32[]{:S(2)}) collective-permute-start(bf16[64,896]{1,0:T(8,128)(2,1)S(1)} %get-tuple-element.39), channel_id=1, source_target_pairs={{0,8},{2,10},{4,12},{6,14},{8,0},{10,2},{12,4},{14,6},{1,9},{3,11}... | collective-permute-start | bytes 344072 | tf_op jit(solution)/shard_map/ppermute | solution.py:331
  167.4 15.7 %collective-permute-start.4 = (bf16[64,896]{1,0:T(8,128)(2,1)S(1)}, bf16[64,896]{1,0:T(8,128)(2,1)S(1)}, u32[]{:S(2)}, u32[]{:S(2)}) collective-permute-start(bf16[64,896]{1,0:T(8,128)(2,1)S(1)} %get-tuple-element.40), channel_id=1, source_target_pairs={{0,10},{2,12},{4,14},{6,0},{8,2},{10,4},{12,6},{14,8},{1,11},{3,13... | collective-permute-start | bytes 344072 | tf_op jit(solution)/shard_map/ppermute | solution.py:331
  171.5 21.4 %collective-permute-start.5 = (bf16[64,896]{1,0:T(8,128)(2,1)S(1)}, bf16[64,896]{1,0:T(8,128)(2,1)S(1)}, u32[]{:S(2)}, u32[]{:S(2)}) collective-permute-start(bf16[64,896]{1,0:T(8,128)(2,1)S(1)} %get-tuple-element.41), channel_id=1, source_target_pairs={{0,12},{2,14},{4,0},{6,2},{8,4},{10,6},{12,8},{14,10},{1,13},{3,15... | collective-permute-start | bytes 344072 | tf_op jit(solution)/shard_map/ppermute | solution.py:331
  176.8 20.8 %collective-permute-start.6 = (bf16[64,896]{1,0:T(8,128)(2,1)S(1)}, bf16[64,896]{1,0:T(8,128)(2,1)S(1)}, u32[]{:S(2)}, u32[]{:S(2)}) collective-permute-start(bf16[64,896]{1,0:T(8,128)(2,1)S(1)} %get-tuple-element.42), channel_id=1, source_target_pairs={{0,14},{2,0},{4,2},{6,4},{8,6},{10,8},{12,10},{14,12},{1,15},{3,1}... | collective-permute-start | bytes 344072 | tf_op jit(solution)/shard_map/ppermute | solution.py:331
  197.6 20.4 %collective-permute-start.7 = (bf16[8,64,896]{2,1,0:T(8,128)(2,1)S(1)}, bf16[8,64,896]{2,1,0:T(8,128)(2,1)}, u32[]{:S(2)}, u32[]{:S(2)}) collective-permute-start(bf16[8,64,896]{2,1,0:T(8,128)(2,1)S(1)} %bitcast_dynamic-update-slice_fusion), channel_id=1, source_target_pairs={{0,1},{1,0},{2,3},{3,2},{4,5},{5,4},{6,7},{7,6},{8,9},{9,8},{10,11... | collective-permute-start | bytes 2752520 | tf_op jit(solution)/shard_map/ppermute | solution.py:346
  219.4 56.5 %copy-start.4 = (s32[64,8]{0,1:T(8,128)S(1)}, s32[64,8]{0,1:T(8,128)}, u32[]{:S(2)}) copy-start(s32[64,8]{0,1:T(8,128)} %param.17) | copy-start | bytes 6148
Sparse Core Ops, SparseCore 0:
  103.1 42.5 all-gather.3
  153.1 59.0 all-gather.5

commit v7 on v6

--- a/solution.py
+++ b/solution.py
@@ -313,7 +313,19 @@
     capacity = own_tokens * routes.shape[1] // expert_count
 
     parts = project(attn_out, out_weight, tensor_count, dp_count)
-    parts = swap(parts.reshape(tensor_count * dp_count, own_tokens // 2, 2 * part), ("tensor", "dp"))
+    parts = swap(
+        parts.reshape(tensor_count * dp_count, own_tokens // 2, 2 * part), ("tensor", "dp")
+    )
+    rolled = list(pack_down(down_weights[0], tensor_count, dp_count))
+    far = range(2, tensor_count - 2)
+    near = [s for s in range(1, tensor_count) if s not in far]
+
+    def roll(s):
+        moves = [(i, (i + s) % tensor_count) for i in range(tensor_count)]
+        return lax.ppermute(rolled[s], "tensor", moves)
+
+    for s in far:
+        rolled[s] = roll(s)
     stream, sent = pl.pallas_call(
         dispatch_kernel,
         out_shape=(
@@ -324,15 +336,12 @@
         name="dispatch",
     )(parts, residual, routes.T)
 
-    packed = pack_down(down_weights[0], tensor_count, dp_count)
-    sent, *packed = lax.optimization_barrier((sent, *packed))
+    sent, *held = lax.optimization_barrier((sent, *[rolled[s] for s in near]))
+    for s, piece in zip(near, held):
+        rolled[s] = piece
     received = swap(sent, "expert")
-    rolled = [
-        lax.ppermute(piece, "tensor", [(i, (i + s) % tensor_count) for i in range(tensor_count)])
-        if s
-        else piece
-        for s, piece in enumerate(packed)
-    ]
+    for s in near:
+        rolled[s] = roll(s)
     received = received.reshape(expert_count, capacity * part)
     whole = lax.all_gather(received, "tensor", axis=0, tiled=False)
     hidden = hidden_units(

time: 286 us -> 287 us (level)
  waiting for transfers between devices: 89.3 us -> 94.7 us
  blocking collectives: 116 us -> 113 us
    ppermute x7, waiting for transfers between devices: 18.5 us -> 21.5 us  [roll(): return lax.ppermute(rolled[s], 'tensor', moves)]
where the time goes in v7:
time: 287 us; the launch traced here: 286 us
  blocking collectives  113 us (39%)
  waiting for transfers between devices  94.7 us (33%)
  starting transfers between devices  35.7 us (12%)
  Pallas kernels  23.3 us (8%)
  between operations  13.7 us (5%)
  local copies, waits for them, and re-layouts  4.14 us (1%)
    all_to_all x2, blocking collectives, swap(): return lax.all_to_all(x, axis, split_axis=0, concat_axis=0, tiled=True)  113 us
    all_gather x1, waiting for transfers between devices, body(): whole = lax.all_gather(received, 'tensor', axis=0, tiled=False)  42.6 us
    ppermute x7, starting transfers between devices, roll(): return lax.ppermute(rolled[s], 'tensor', moves)  23.8 us
    ppermute x7, waiting for transfers between devices, roll(): return lax.ppermute(rolled[s], 'tensor', moves)  21.5 us
    ppermute x1, waiting for transfers between devices, body(): theirs = lax.ppermute(mine, 'dp', [(0, 1), (1, 0)])  19.7 us
    all_to_all x1, waiting for transfers between devices, swap(): return lax.all_to_all(x, axis, split_axis=0, concat_axis=0, tiled=True)  10.7 us
    all_to_all x1, starting transfers between devices, swap(): return lax.all_to_all(x, axis, split_axis=0, concat_axis=0, tiled=True)  8.8 us
    pallas_call x1, Pallas kernels, hidden_units(): pl.pallas_call(functools.partial(hidden_kernel, steps), grid=(steps,), in...  7.3 us
  transfers between devices with their start and end apart: 11, of which 6 were waited for; matrix products, arithmetic and copies ran while one was open for 1% of the time, Pallas kernels for 1%

profile of v7, /device:TPU:1, one launch (start us, length us, event | category | flops | bytes accessed | tf_op | source)
XLA Modules:
  0.0 286.1 jit_solution(2404094327334162615)
XLA Ops:
  7.4 4.6 %project.1 = bf16[8,2,32,896]{3,2,1,0:T(8,128)(2,1)} custom-call(bf16[128,512]{1,0:T(8,128)(2,1)S(1)} %copy-done.1, bf16[512,3584]{1,0:T(8,128)(2,1)} %weight_ref.1), custom_call_target="tpu_custom_call" | custom-call | tf_op jit(solution)/shard_map/project/pallas_call | solution.py:41
  12.0 8.8 %all-to-all-start = ((bf16[16,32,896]{2,1,0:T(8,128)(2,1)}), bf16[16,32,896]{2,1,0:T(8,128)(2,1)S(1)}, u32[]{:S(2)}, u32[]{:S(2)}) async-start(bf16[16,32,896]{2,1,0:T(8,128)(2,1)} %bitcast), calls=%async_computation | async-start | bytes 1835008 | tf_op jit(solution)/shard_map/all_to_all | solution.py:294
  20.9 3.2 %pack_down.1 = (bf16[64,896]{1,0:T(8,128)(2,1)S(1)}, bf16[64,896]{1,0:T(8,128)(2,1)S(1)}, bf16[64,896]{1,0:T(8,128)(2,1)S(1)}, bf16[64,896]{1,0:T(8,128)(2,1)S(1...) custom-call(s32[2]{0:T(128)S(1)} %pad_add_fusion.rank_ref, ...), custom_call_target="tpu_custom_call" | custom-call | tf_op jit(solution)/shard_map/pack_down/pallas_call | solution.py:110
  26.1 10.7 %all-to-all-done.parts_ref = bf16[16,32,896]{2,1,0:T(8,128)(2,1)S(1)} async-done(((bf16[16,32,896]{2,1,0:T(8,128)(2,1)}), bf16[16,32,896]{2,1,0:T(8,128)(2,1)S(1)}, u32[]{:S(2)}, u32[]{:S(2)}) %all-to-all-start) | async-done | bytes 917536 | tf_op jit(solution)/shard_map/all_to_all | solution.py:294
  36.9 1.2 dispatch.1
  38.0 63.8 %all_to_all.15 = bf16[64,2,1792]{2,1,0:T(2,128)(2,1)S(1)} all-to-all(bf16[64,2,1792]{2,1,0:T(2,128)(2,1)S(1)} %get-tuple-element.24), channel_id=1, replica_groups=mesh['expert'=64,'tensor'=8,'dp'=2] {'expert'}, dimensions={0} | all-to-all | bytes 917504 | tf_op jit(solution)/shard_map/all_to_all | solution.py:294
  103.1 42.6 %all-gather.4.cloned.1.call-done.x_ref = bf16[8,64,3584]{2,1,0:T(8,128)(2,1)} async-done(((bf16[1,64,3584]{2,1,0:T(8,128)(2,1)}), bf16[8,64,3584]{2,1,0:T(8,128)(2,1)}) %all-gather.4.cloned.1.call-update) | async-done | bytes 3670032 | tf_op jit(solution)/shard_map/all_gather | solution.py:346
  145.7 7.3 %hidden_units.1 = bf16[512,256]{1,0:T(8,128)(2,1)} custom-call(bf16[8,64,3584]{2,1,0:T(8,128)(2,1)} %all-gather.4.cloned.1.call-done.x_ref, f32[8,1,448]{2,1,0:T(1,128)S(1)} %reshape.11.gain_ref, bf16[3584,256]{1,0:T(8,128)(2,1)S(1)} %bitcast.25, bf16[3584,256]{1,0:T(8,128)(2,1)} %bitcast.32), custom_call_target="tpu_custom_call" | custom-call | tf_op jit(solution)/shard_map/hidden_units/pallas_call | solution.py:183
  153.0 2.9 %collective-permute-start.1 = (bf16[64,896]{1,0:T(8,128)(2,1)S(1)}, bf16[64,896]{1,0:T(8,128)(2,1)S(1)}, u32[]{:S(2)}, u32[]{:S(2)}) collective-permute-start(bf16[64,896]{1,0:T(8,128)(2,1)S(1)} %copy-done.8), channel_id=1, source_target_pairs={{0,4},{2,6},{4,8},{6,10},{8,12},{10,14},{12,0},{14,2},{1,5},{3,7},... | collective-permute-start | bytes 344072 | tf_op jit(solution)/shard_map/ppermute | solution.py:325
  156.0 5.0 %collective-permute-start.2 = (bf16[64,896]{1,0:T(8,128)(2,1)S(1)}, bf16[64,896]{1,0:T(8,128)(2,1)S(1)}, u32[]{:S(2)}, u32[]{:S(2)}) collective-permute-start(bf16[64,896]{1,0:T(8,128)(2,1)S(1)} %copy-done.6), channel_id=1, source_target_pairs={{0,6},{2,8},{4,10},{6,12},{8,14},{10,0},{12,2},{14,4},{1,7},{3,9},... | collective-permute-start | bytes 344072 | tf_op jit(solution)/shard_map/ppermute | solution.py:325
  161.0 2.5 collective-permute-start.3
  163.5 5.8 %collective-permute-start.4 = (bf16[64,896]{1,0:T(8,128)(2,1)S(1)}, bf16[64,896]{1,0:T(8,128)(2,1)S(1)}, u32[]{:S(2)}, u32[]{:S(2)}) collective-permute-start(bf16[64,896]{1,0:T(8,128)(2,1)S(1)} %get-tuple-element.30), channel_id=1, source_target_pairs={{0,10},{2,12},{4,14},{6,0},{8,2},{10,4},{12,6},{14,8},{1,11},{3,13... | collective-permute-start | bytes 344072 | tf_op jit(solution)/shard_map/ppermute | solution.py:325
  169.3 2.2 collective-permute-start
  171.5 9.8 %collective-permute-done = bf16[64,896]{1,0:T(8,128)(2,1)S(1)} collective-permute-done((bf16[64,896]{1,0:T(8,128)(2,1)S(1)}, bf16[64,896]{1,0:T(8,128)(2,1)S(1)}, u32[]{:S(2)}, u32[]{:S(2)}) %collective-permute-start) | collective-permute-done | bytes 114720 | tf_op jit(solution)/shard_map/ppermute | solution.py:325
  181.4 2.1 collective-permute-start.5
  183.5 3.2 %collective-permute-start.6 = (bf16[64,896]{1,0:T(8,128)(2,1)S(1)}, bf16[64,896]{1,0:T(8,128)(2,1)S(1)}, u32[]{:S(2)}, u32[]{:S(2)}) collective-permute-start(bf16[64,896]{1,0:T(8,128)(2,1)S(1)} %get-tuple-element.32), channel_id=1, source_target_pairs={{0,14},{2,0},{4,2},{6,4},{8,6},{10,8},{12,10},{14,12},{1,15},{3,1}... | collective-permute-start | bytes 344072 | tf_op jit(solution)/shard_map/ppermute | solution.py:325
  186.9 6.9 %collective-permute-done.5 = bf16[64,896]{1,0:T(8,128)(2,1)S(1)} collective-permute-done((bf16[64,896]{1,0:T(8,128)(2,1)S(1)}, bf16[64,896]{1,0:T(8,128)(2,1)S(1)}, u32[]{:S(2)}, u32[]{:S(2)}) %collective-permute-start.5) | collective-permute-done | bytes 114720 | tf_op jit(solution)/shard_map/ppermute | solution.py:325
  193.8 4.8 %collective-permute-done.6 = bf16[64,896]{1,0:T(8,128)(2,1)S(1)} collective-permute-done((bf16[64,896]{1,0:T(8,128)(2,1)S(1)}, bf16[64,896]{1,0:T(8,128)(2,1)S(1)}, u32[]{:S(2)}, u32[]{:S(2)}) %collective-permute-start.6) | collective-permute-done | bytes 114720 | tf_op jit(solution)/shard_map/ppermute | solution.py:325
  198.6 3.1 %collective-permute-start.7 = (bf16[8,64,896]{2,1,0:T(8,128)(2,1)S(1)}, bf16[8,64,896]{2,1,0:T(8,128)(2,1)}, u32[]{:S(2)}, u32[]{:S(2)}) collective-permute-start(bf16[8,64,896]{2,1,0:T(8,128)(2,1)S(1)} %bitcast_dynamic-update-slice_fusion), channel_id=1, source_target_pairs={{0,1},{1,0},{2,3},{3,2},{4,5},{5,4},{6,7},{7,6},{8,9},{9,8},{10,11... | collective-permute-start | bytes 2752520 | tf_op jit(solution)/shard_map/ppermute | solution.py:355
  201.7 19.7 %collective-permute-done.7 = bf16[8,64,896]{2,1,0:T(8,128)(2,1)} collective-permute-done((bf16[8,64,896]{2,1,0:T(8,128)(2,1)S(1)}, bf16[8,64,896]{2,1,0:T(8,128)(2,1)}, u32[]{:S(2)}, u32[]{:S(2)}) %collective-permute-start.7) | collective-permute-done | bytes 917536 | tf_op jit(solution)/shard_map/ppermute | solution.py:355
  221.5 1.4 broadcast_select_fusion
  222.8 4.8 %expert_outputs.1 = bf16[64,2,1792]{2,1,0:T(2,128)(2,1)S(1)} custom-call(s32[1]{0:T(128)} %bitcast.3.rank_ref, bf16[8,512,256]{2,1,0:T(8,128)(2,1)} %bitcast.29, bf16[8,512,256]{2,1,0:T(8,128)(2,1)} %bitcast.30, bf16[8,64,896]{2,1,0:T(8,128)(2,1)S(1)} %get-tuple-element.34.low_ref, bf16[8,64,896]{2,1,0:T(8,128)(2,1)S(1)} %get-tuple-element.33.high_ref), custom_call_target="tpu_custom_call" | custom-call | tf_op jit(solution)/shard_map/expert_outputs/pallas_call | solution.py:255
  227.6 49.4 %all_to_all.16.returned_ref = bf16[64,2,1792]{2,1,0:T(2,128)(2,1)S(1)} all-to-all(bf16[64,2,1792]{2,1,0:T(2,128)(2,1)S(1)} %expert_outputs.1), channel_id=1, replica_groups=mesh['expert'=64,'tensor'=8,'dp'=2] {'expert'}, dimensions={0} | all-to-all | bytes 917504 | tf_op jit(solution)/shard_map/all_to_all | solution.py:294
  277.0 2.2 combine.1
  (44 shorter events, 4.4 us)
Async XLA Ops:
  6.5 0.9 copy-start.1
  12.0 24.9 %copy-start.2 = (bf16[64,448]{1,0:T(8,128)(2,1)S(1)}, bf16[64,448]{1,0:T(8,128)(2,1)}, u32[]{:S(2)}) copy-start(bf16[64,448]{1,0:T(8,128)(2,1)} %residual_ref.1) | copy-start | bytes 172036
  12.0 24.9 %copy-start.3 = (s32[64,8]{0,1:T(8,128)S(1)}, s32[64,8]{0,1:T(8,128)}, u32[]{:S(2)}) copy-start(s32[64,8]{0,1:T(8,128)} %param.16) | copy-start | bytes 6148
  12.0 24.8 %all-to-all-start = ((bf16[16,32,896]{2,1,0:T(8,128)(2,1)}), bf16[16,32,896]{2,1,0:T(8,128)(2,1)S(1)}, u32[]{:S(2)}, u32[]{:S(2)}) async-start(bf16[16,32,896]{2,1,0:T(8,128)(2,1)} %bitcast), calls=%async_computation | async-start | bytes 1835008 | tf_op jit(solution)/shard_map/all_to_all | solution.py:294
  20.8 124.9 %all-gather.4.cloned.1.call-start = ((), (), s32[]{:S(2)}) async-start(), calls=%async_computation.3 | async-start | bytes 4128768 | tf_op jit(solution)/shard_map/all_gather | solution.py:346
  24.2 0.7 copy-start.5
  24.8 0.6 copy-start.7
  25.5 0.7 copy-start.9
  26.1 76.9 %copy-start.11 = (f32[3584]{0:T(1024)S(1)}, f32[3584]{0:T(1024)}, u32[]{:S(2)}) copy-start(f32[3584]{0:T(1024)} %param.12) | copy-start | bytes 43012
  26.1 119.5 %copy-start = (bf16[1,3584,256]{2,1,0:T(8,128)(2,1)S(1)}, bf16[1,3584,256]{2,1,0:T(8,128)(2,1)}, u32[]{:S(2)}) copy-start(bf16[1,3584,256]{2,1,0:T(8,128)(2,1)} %param.13) | copy-start | bytes 5505028
  102.9 119.9 %all-gather.6.cloned.1.call-start = ((), (), s32[]{:S(2)}) async-start(), calls=%async_computation.4 | async-start | bytes 2359296 | tf_op jit(solution)/shard_map/all_gather | solution.py:353
  145.7 7.3 %copy-start.8 = (bf16[64,896]{1,0:T(8,128)(2,1)S(1)}, bf16[64,896]{1,0:T(8,128)(2,1)}, u32[]{:S(2)}) copy-start(bf16[64,896]{1,0:T(8,128)(2,1)} %copy-done.7) | copy-start | bytes 344068
  145.7 10.3 %copy-start.6 = (bf16[64,896]{1,0:T(8,128)(2,1)S(1)}, bf16[64,896]{1,0:T(8,128)(2,1)}, u32[]{:S(2)}) copy-start(bf16[64,896]{1,0:T(8,128)(2,1)} %copy-done.5) | copy-start | bytes 344068
  145.7 23.6 %copy-start.10 = (bf16[64,896]{1,0:T(8,128)(2,1)S(1)}, bf16[64,896]{1,0:T(8,128)(2,1)}, u32[]{:S(2)}) copy-start(bf16[64,896]{1,0:T(8,128)(2,1)} %copy-done.9) | copy-start | bytes 344068
  153.0 30.5 %collective-permute-start.1 = (bf16[64,896]{1,0:T(8,128)(2,1)S(1)}, bf16[64,896]{1,0:T(8,128)(2,1)S(1)}, u32[]{:S(2)}, u32[]{:S(2)}) collective-permute-start(bf16[64,896]{1,0:T(8,128)(2,1)S(1)} %copy-done.8), channel_id=1, source_target_pairs={{0,4},{2,6},{4,8},{6,10},{8,12},{10,14},{12,0},{14,2},{1,5},{3,7},... | collective-permute-start | bytes 344072 | tf_op jit(solution)/shard_map/ppermute | solution.py:325
  156.0 30.8 %collective-permute-start.2 = (bf16[64,896]{1,0:T(8,128)(2,1)S(1)}, bf16[64,896]{1,0:T(8,128)(2,1)S(1)}, u32[]{:S(2)}, u32[]{:S(2)}) collective-permute-start(bf16[64,896]{1,0:T(8,128)(2,1)S(1)} %copy-done.6), channel_id=1, source_target_pairs={{0,6},{2,8},{4,10},{6,12},{8,14},{10,0},{12,2},{14,4},{1,7},{3,9},... | collective-permute-start | bytes 344072 | tf_op jit(solution)/shard_map/ppermute | solution.py:325
  161.0 25.8 %collective-permute-start.3 = (bf16[64,896]{1,0:T(8,128)(2,1)S(1)}, bf16[64,896]{1,0:T(8,128)(2,1)S(1)}, u32[]{:S(2)}, u32[]{:S(2)}) collective-permute-start(bf16[64,896]{1,0:T(8,128)(2,1)S(1)} %get-tuple-element.29), channel_id=1, source_target_pairs={{0,8},{2,10},{4,12},{6,14},{8,0},{10,2},{12,4},{14,6},{1,9},{3,11}... | collective-permute-start | bytes 344072 | tf_op jit(solution)/shard_map/ppermute | solution.py:325
  163.5 23.4 %collective-permute-start.4 = (bf16[64,896]{1,0:T(8,128)(2,1)S(1)}, bf16[64,896]{1,0:T(8,128)(2,1)S(1)}, u32[]{:S(2)}, u32[]{:S(2)}) collective-permute-start(bf16[64,896]{1,0:T(8,128)(2,1)S(1)} %get-tuple-element.30), channel_id=1, source_target_pairs={{0,10},{2,12},{4,14},{6,0},{8,2},{10,4},{12,6},{14,8},{1,11},{3,13... | collective-permute-start | bytes 344072 | tf_op jit(solution)/shard_map/ppermute | solution.py:325
  169.3 12.1 %collective-permute-start = (bf16[64,896]{1,0:T(8,128)(2,1)S(1)}, bf16[64,896]{1,0:T(8,128)(2,1)S(1)}, u32[]{:S(2)}, u32[]{:S(2)}) collective-permute-start(bf16[64,896]{1,0:T(8,128)(2,1)S(1)} %copy-done.10), channel_id=1, source_target_pairs={{0,2},{2,4},{4,6},{6,8},{8,10},{10,12},{12,14},{14,0},{1,3},{3,5},... | collective-permute-start | bytes 344072 | tf_op jit(solution)/shard_map/ppermute | solution.py:325
  181.4 12.4 %collective-permute-start.5 = (bf16[64,896]{1,0:T(8,128)(2,1)S(1)}, bf16[64,896]{1,0:T(8,128)(2,1)S(1)}, u32[]{:S(2)}, u32[]{:S(2)}) collective-permute-start(bf16[64,896]{1,0:T(8,128)(2,1)S(1)} %get-tuple-element.31), channel_id=1, source_target_pairs={{0,12},{2,14},{4,0},{6,2},{8,4},{10,6},{12,8},{14,10},{1,13},{3,15... | collective-permute-start | bytes 344072 | tf_op jit(solution)/shard_map/ppermute | solution.py:325
  183.5 15.1 %collective-permute-start.6 = (bf16[64,896]{1,0:T(8,128)(2,1)S(1)}, bf16[64,896]{1,0:T(8,128)(2,1)S(1)}, u32[]{:S(2)}, u32[]{:S(2)}) collective-permute-start(bf16[64,896]{1,0:T(8,128)(2,1)S(1)} %get-tuple-element.32), channel_id=1, source_target_pairs={{0,14},{2,0},{4,2},{6,4},{8,6},{10,8},{12,10},{14,12},{1,15},{3,1}... | collective-permute-start | bytes 344072 | tf_op jit(solution)/shard_map/ppermute | solution.py:325
  198.6 22.8 %collective-permute-start.7 = (bf16[8,64,896]{2,1,0:T(8,128)(2,1)S(1)}, bf16[8,64,896]{2,1,0:T(8,128)(2,1)}, u32[]{:S(2)}, u32[]{:S(2)}) collective-permute-start(bf16[8,64,896]{2,1,0:T(8,128)(2,1)S(1)} %bitcast_dynamic-update-slice_fusion), channel_id=1, source_target_pairs={{0,1},{1,0},{2,3},{3,2},{4,5},{5,4},{6,7},{7,6},{8,9},{9,8},{10,11... | collective-permute-start | bytes 2752520 | tf_op jit(solution)/shard_map/ppermute | solution.py:355
  222.8 54.2 %copy-start.4 = (s32[64,8]{0,1:T(8,128)S(1)}, s32[64,8]{0,1:T(8,128)}, u32[]{:S(2)}) copy-start(s32[64,8]{0,1:T(8,128)} %param.17) | copy-start | bytes 6148
Sparse Core Ops, SparseCore 0:
  103.1 42.5 all-gather.3
  153.1 55.4 all-gather.5
